TPU v7x, 128 devices: a whole 4x4x4 slice. The times are simulated.
128 devices in a mesh: grp: 2 (over z_hi), tile: 32 (over x, y, core), spec: 2 (over z_lo).
Axes of the slice: x: 4, y: 4, z: 4 (z_hi: 2, z_lo: 2; z = z_hi * 2 + z_lo), core: 2. Of those that a mesh axis runs over, the one named last changes fastest.
Arguments:
- spectrum: float32 [2, 32, 36, 256, 256], P('grp', None, 'spec', 'tile'), may hold values from 0.01 to 1
- wind: float32 [2, 256, 256], P(None, 'tile'), may hold values from -48 to 48
- land_mask: int32 [256, 256], P('tile'), may hold values 0 or 1
- intersection: int32 [256, 256], P('tile'), may hold values from 0 to 255, as said below
- ocean_state: float32 [2, 3, 16, 256, 256], P('grp', None, 'spec', 'tile'), may hold values from -1 to 1
- sea_level: float32 [2, 256, 256], P('grp', 'tile'), may hold values from -1 to 1
Outputs:
- spectrum_next: float32 [2, 32, 36, 256, 256], P('grp', None, 'spec', 'tile')
- ocean_next: float32 [2, 3, 16, 256, 256], P('grp', None, 'spec', 'tile')
Inputs may be any that keep to these rules, and one draw needn't show every extreme that they name: In each row i, intersection[i, j] = (j + s_i) mod 256 for a shift s_i of that row.
All inputs are finite; a program needn't handle non-finite values. No bound on the sum of `land_mask` on one device may be relied on, other than what follows from the above.
Results may differ from a plain program's by a relative error of at most 0.0001.
Values sent between devices are 32-bit elements; how exact they have to be, the bound alone decides.
A program may use at most 128 MiB of HBM per device.

v0:
```python
import math

import jax
import jax.numpy as jnp
import numpy as np
from jax import lax
from jax.experimental import pallas as pl
from jax.experimental.pallas import tpu as pltpu
from jax.sharding import PartitionSpec as P

FREQS = 32
DIRS = 36
LEVELS = 16
WSTEPS = 4
TILES = 32
DLOC = 18
KLOC = 8
FD = FREQS * DLOC
CHUNKS = 8
FCH = FREQS // CHUNKS
RCH = FCH * DLOC
F32 = jnp.float32

_freq = 0.04 * 1.1 ** np.arange(FREQS)
_cel = 1.56 / _freq
_gs = 0.4 * 1.1 ** (-np.arange(FREQS, dtype=np.float64))
_bw = 0.1 * _freq * (2.0 * math.pi / DIRS)
TABLE = np.stack([_gs, 0.05 / _cel, _bw, 5.0 * _bw / _cel, 20.0 * _bw * _freq**3]).astype(np.float32)
_ang = 2.0 * math.pi * (np.arange(DIRS) + 0.5) / DIRS
COS = [float(np.float32(x)) for x in np.cos(_ang)[:DLOC]]
SIN = [float(np.float32(x)) for x in np.sin(_ang)[:DLOC]]
_prof = np.exp(-2.0 * (np.arange(LEVELS) + 0.5) / LEVELS)
_wgt = _prof / _prof.sum()


def mesh_copy(src, dst, send, recv, where):
    return pltpu.make_async_remote_copy(
        src_ref=src,
        dst_ref=dst,
        send_sem=send,
        recv_sem=recv,
        device_id=where,
        device_id_type=pl.DeviceIdType.MESH,
    )


def settle(buf, sem):
    pltpu.make_async_copy(buf, buf, sem).wait()


def kernel(
    tab, spec_h, wind_h, land_h, inter_h, ocean_h, sea_h, out_w, out_o,
    B, G, WD, CNT, H, S, wind, land, inter, NBS, NBR, QR, TS, TR, BANDS, BANDR, MSG2, MMSG,
    Q, A1, A2, sea, CS, CR, SX, MSG, MR, BR, BTS, ES, EH, LS, LH, zbuf,
    load_sem, small_sem, h_send, h_recv, t_send, t_recv, nb_send, nb_recv,
    q_send, q_recv, m_send, m_recv, f_send, f_recv, c_send, c_recv, e_send, e_recv, l_send, l_recv, out_sem,
):
    grp = lax.axis_index("grp")
    tile = lax.axis_index("tile")
    sp = lax.axis_index("spec")
    other = 1 - sp
    sgn = (1 - 2 * sp).astype(F32)
    has_lo = tile > 0
    has_hi = tile < TILES - 1
    lo_t = jnp.maximum(tile - 1, 0)
    hi_t = jnp.minimum(tile + 1, TILES - 1)
    lane = lax.broadcasted_iota(jnp.int32, (8, 128), 1)
    row = lax.broadcasted_iota(jnp.int32, (8, 128), 0)
    first_lane, last_lane = lane == 0, lane == 127
    first_row, last_row = row == 0, row == 7
    low_rows = row < 4
    halves = (slice(0, 128), slice(128, 256))

    def from_left(x):
        a, b = pltpu.roll(x[0], 1, 1), pltpu.roll(x[1], 1, 1)
        return jnp.where(first_lane, 0.0, a), jnp.where(first_lane, a, b)

    def from_right(x):
        a, b = pltpu.roll(x[0], 127, 1), pltpu.roll(x[1], 127, 1)
        return jnp.where(last_lane, b, a), jnp.where(last_lane, 0.0, b)

    def circular(x, shift):
        a, b = pltpu.roll(x[0], shift, 1), pltpu.roll(x[1], shift, 1)
        m = lane < shift
        return jnp.where(m, b, a), jnp.where(m, a, b)

    def barrel(x, amount):
        for bit in range(8):
            moved = circular(x, 1 << bit) if bit < 7 else (x[1], x[0])
            x = tuple(jnp.where((amount[h] & (1 << bit)) != 0, moved[h], x[h]) for h in range(2))
        return x

    def pair(ref, *lead):
        return tuple(ref[(*lead, slice(None), hs)] for hs in halves)

    def put(ref, value, rows):
        for h in range(2):
            ref[rows, halves[h]] = value[h]

    @pl.when(grp == 0)
    def wave():
        def load(c):
            rows = pl.ds(pl.multiple_of(c * RCH * 8, 8), RCH * 8)
            return [
                pltpu.make_async_copy(spec_h.at[rows, hs], B.at[h, rows, :], load_sem.at[c, h])
                for h, hs in enumerate(halves)
            ]

        smalls = [
            pltpu.make_async_copy(wind_h, wind, small_sem.at[0]),
            pltpu.make_async_copy(land_h, land, small_sem.at[1]),
            pltpu.make_async_copy(inter_h, inter, small_sem.at[2]),
        ]
        for copy in smalls:
            copy.start()

        def begin(c, carry):
            for copy in load(c):
                copy.start()
            return carry

        lax.fori_loop(0, CHUNKS, begin, 0)

        def halo(n, side, c):
            rows = pl.ds(pl.multiple_of(c * RCH, 8), RCH)
            return mesh_copy(
                S.at[n, side, :, rows, :], H.at[n, side, :, rows, :], h_send.at[n, side, c], h_recv.at[n, side, c],
                {"tile": hi_t if side == 0 else lo_t},
            )

        def edges_out(n, c):
            for k in range(RCH // 8):
                at = c * RCH + 8 * k
                rows = pl.ds(pl.multiple_of(at, 8), 8)
                for h in range(2):
                    S[n, 0, h, rows, :] = B[h, pl.ds(at * 8 + 7, 8, stride=8), :]
                    S[n, 1, h, rows, :] = B[h, pl.ds(at * 8, 8, stride=8), :]

            @pl.when(has_hi)
            def _():
                halo(n, 0, c).start()

            @pl.when(has_lo)
            def _():
                halo(n, 1, c).start()

        for copy in smalls:
            copy.wait()
        wet_i = pair(land)
        wet = tuple(x.astype(F32) for x in wet_i)
        shift = tuple((x - lane - 128 * h) & 255 for h, x in enumerate(pair(inter)))
        put(NBS, wet_i, slice(0, 8))
        put(NBS, shift, slice(8, 16))

        def neighbour(side):
            return mesh_copy(
                NBS, NBR.at[side], nb_send.at[side], nb_recv.at[side],
                {"tile": hi_t if side == 0 else lo_t},
            )

        @pl.when(has_hi)
        def _():
            neighbour(0).start()

        @pl.when(has_lo)
        def _():
            neighbour(1).start()

        wet_back = circular(barrel(wet, shift), 1)

        def windows(fields, u):
            acc = jnp.zeros((8, 128), F32)
            for f, field in enumerate(fields):
                start = (8 * u + 32 * f) % 128
                offset = (lane - start) & 127
                inside = offset < 10
                base = (8 * u) // 128
                p = 8 * u + offset
                value = field[base]
                if 8 * u % 128 + 10 > 128:
                    turned = (lane - 32 * f) & 127
                    value = jnp.where(turned < 16, field[1 - base], value)
                acc = jnp.where(inside, value, acc)
            return acc

        for u in range(TILES):
            MMSG[pl.ds(8 * u, 8), :] = windows([wet_back], u)

        def to_ocean(src, dst, send, recv, u):
            return mesh_copy(
                src.at[pl.ds(pl.multiple_of(u * 8, 8), 8), :],
                dst.at[pl.ds(pl.multiple_of(tile * 8, 8), 8), :],
                send, recv, {"grp": 1, "tile": u},
            )

        def send_mask(u, carry):
            to_ocean(MMSG, MR, m_send, m_recv, u).start()
            return carry

        lax.fori_loop(0, TILES, send_mask, 0)

        @pl.when(jnp.logical_not(has_lo))
        def _():
            H[:, 0] = jnp.zeros((WSTEPS, 2, FD, 128), F32)
            NBR[0] = jnp.zeros((16, 256), jnp.int32)
            TR[:, 1:3] = jnp.zeros((WSTEPS, 2, 8, 256), F32)

        @pl.when(jnp.logical_not(has_hi))
        def _():
            H[:, 1] = jnp.zeros((WSTEPS, 2, FD, 128), F32)
            NBR[1] = jnp.zeros((16, 256), jnp.int32)
            TR[:, 3:5] = jnp.zeros((WSTEPS, 2, 8, 256), F32)

        def first_edges(c, carry):
            for copy in load(c):
                copy.wait()
            edges_out(0, c)
            return carry

        lax.fori_loop(0, CHUNKS, first_edges, 0)

        for d in range(DLOC):
            for h, hs in enumerate(halves):
                WD[d, :, hs] = wind[0, :, hs] * (sgn * COS[d]) + wind[1, :, hs] * (sgn * SIN[d])

        def growth(f, carry):
            slope = tab[1, f]
            sgs = tab[0, f] * sgn
            for d in range(DLOC):
                i = f * DLOC + d
                rows = pl.ds(pl.multiple_of(i * 8, 8), 8)
                for h, hs in enumerate(halves):
                    G[h, rows, :] = 1.0 + jnp.maximum(WD[d, :, hs] * slope - 0.05, 0.0)
                CNT[pl.ds(i, 1), :] = jnp.full((1, 128), sgs * SIN[d], F32)
            return carry

        lax.fori_loop(0, FREQS, growth, 0)

        @pl.when(has_lo)
        def _():
            neighbour(0).wait_recv()

        @pl.when(has_hi)
        def _():
            neighbour(1).wait_recv()

        edge_i = tuple(
            jnp.where(low_rows, NBR[1, 0:8, hs], NBR[0, 0:8, hs]) for hs in halves
        )
        edge_wet = tuple(x.astype(F32) for x in edge_i)
        edge_shift = tuple(
            jnp.where(low_rows, NBR[1, 8:16, hs], NBR[0, 8:16, hs]) for hs in halves
        )

        settle(QR, q_recv)
        fields = []
        for c in range(5):
            parts = []
            for h in range(2):
                acc = jnp.zeros((8, 128), F32)
                for k in range(16):
                    u = 16 * h + k
                    acc = jnp.where((lane >> 3) == (k + c) % 16, QR[pl.ds(8 * u, 8), :], acc)
                parts.append(pltpu.roll(acc, 128 - 8 * c, 1) if c else acc)
            fields.append(tuple(parts))
        left = tuple((256 - x) & 255 for x in shift)
        edge_left = tuple((256 - x) & 255 for x in edge_shift)
        u01 = tuple(0.1 * x for x in barrel(fields[0], left))
        v01 = tuple(0.1 * x for x in barrel(fields[1], left))

        def stiffness(level):
            depth = tuple(10.0 + 4.0 * x for x in level)
            return tuple(25.0 / (x * x) for x in depth)

        stiff = stiffness(barrel(fields[2], left))
        edge_v = tuple(0.1 * x for x in barrel(fields[3], edge_left))
        edge_stiff = stiffness(barrel(fields[4], edge_left))
        v_lo = tuple(jnp.broadcast_to(x[7:8], (8, 128)) for x in edge_v)
        v_hi = tuple(jnp.broadcast_to(x[0:1], (8, 128)) for x in edge_v)

        def sweep(n, r, edge_r, last):
            r_lo = tuple(jnp.broadcast_to(x[7:8], (8, 128)) for x in edge_r)
            r_hi = tuple(jnp.broadcast_to(x[0:1], (8, 128)) for x in edge_r)

            def chunk(c, sums):
                @pl.when(has_lo)
                def _():
                    halo(n, 0, c).wait_recv()

                @pl.when(has_hi)
                def _():
                    halo(n, 1, c).wait_recv()

                for k in range(RCH // 8):
                    rows = pl.ds(pl.multiple_of(c * RCH + 8 * k, 8), 8)
                    cn = CNT[rows, :]
                    for h in range(2):
                        H[n, 0, h, rows, :] = jnp.maximum((cn + v_lo[h]) * (r_lo[h] * H[n, 0, h, rows, :]), 0.0)
                        H[n, 1, h, rows, :] = jnp.minimum((cn + v_hi[h]) * (r_hi[h] * H[n, 1, h, rows, :]), 0.0)

                def band(fc, sums):
                    f = c * FCH + fc
                    sgs = tab[0, f] * sgn
                    slope = tab[1, f]
                    zero = jnp.zeros((8, 128), F32)
                    acc = [[zero, zero] for _ in range(5 if last else 1)]
                    for d in range(DLOC):
                        i = f * DLOC + d
                        rows = pl.ds(pl.multiple_of(i * 8, 8), 8)
                        ce = sgs * COS[d]
                        cn = sgs * SIN[d]
                        E = [r[h] * B[h, rows, :] for h in range(2)]
                        X = [(u01[h] + ce) * E[h] for h in range(2)]
                        Y = [(v01[h] + cn) * E[h] for h in range(2)]
                        west = from_left([jnp.maximum(x, 0.0) for x in X])
                        east = from_right([jnp.minimum(x, 0.0) for x in X])
                        for h, hs in enumerate(halves):
                            south = jnp.where(
                                first_row,
                                H[n, 0, h, pl.ds(i, 8, stride=0), :],
                                pltpu.roll(jnp.maximum(Y[h], 0.0), 1, 0),
                            )
                            north = jnp.where(
                                last_row,
                                H[n, 1, h, pl.ds(i, 8, stride=0), :],
                                pltpu.roll(jnp.minimum(Y[h], 0.0), 7, 0),
                            )
                            adv = ((E[h] - jnp.abs(X[h])) - jnp.abs(Y[h])) + (
                                (west[h] - east[h]) + (south - north)
                            )
                            new = adv * G[h, rows, :]
                            B[h, rows, :] = new
                            acc[0][h] += adv
                            if last:
                                push = adv * jnp.maximum(WD[d, :, hs] * slope - 0.05, 0.0)
                                acc[1][h] += push * COS[d]
                                acc[2][h] += push * SIN[d]
                                acc[3][h] += new * COS[d]
                                acc[4][h] += new * SIN[d]
                    weights = [tab[2, f], tab[3, f], tab[3, f], tab[4, f], tab[4, f]]
                    if last:
                        weights = weights[:1] + [w * sgn for w in weights[1:]]
                    return tuple(
                        tuple(total[h] + acc[q][h] * weights[q] for h in range(2)) for q, total in enumerate(sums)
                    )

                sums = lax.fori_loop(0, FCH, band, sums)
                if not last:
                    edges_out(n + 1, c)
                return sums

            zero = jnp.zeros((8, 128), F32)
            init = tuple((zero, zero) for _ in range(5 if last else 1))
            return lax.fori_loop(0, CHUNKS, chunk, init)

        def total_copies(n):
            return [
                (None, mesh_copy(TS.at[n], TR.at[n, 0], t_send.at[n, 0], t_recv.at[n, 0], {"spec": other})),
                (has_hi, mesh_copy(TS.at[n], TR.at[n, 1], t_send.at[n, 1], t_recv.at[n, 1], {"tile": hi_t})),
                (has_hi, mesh_copy(TS.at[n], TR.at[n, 2], t_send.at[n, 2], t_recv.at[n, 2], {"tile": hi_t, "spec": other})),
                (has_lo, mesh_copy(TS.at[n], TR.at[n, 3], t_send.at[n, 3], t_recv.at[n, 3], {"tile": lo_t})),
                (has_lo, mesh_copy(TS.at[n], TR.at[n, 4], t_send.at[n, 4], t_recv.at[n, 4], {"tile": lo_t, "spec": other})),
            ]

        def gated(condition, action):
            if condition is None:
                action()
            else:
                pl.when(condition)(action)

        def one_step(n, carry):
            r, edge_r = carry
            (total,) = sweep(n, r, edge_r, False)
            for h, hs in enumerate(halves):
                TS[n, :, hs] = total[h]
            copies = total_copies(n)
            for condition, copy in copies:
                gated(condition, copy.start)
            for (_, copy), condition in zip(copies, [None, has_lo, has_lo, has_hi, has_hi]):
                gated(condition, copy.wait_recv)
            new_r, new_edge = [], []
            for h, hs in enumerate(halves):
                full = total[h] + TR[n, 0, :, hs]
                new_r.append(wet[h] / (1.0 + stiff[h] * full))
                lower = TR[n, 1, :, hs] + TR[n, 2, :, hs]
                upper = TR[n, 3, :, hs] + TR[n, 4, :, hs]
                edge = jnp.where(low_rows, upper, lower)
                new_edge.append(edge_wet[h] / (1.0 + edge_stiff[h] * edge))
            return tuple(new_r), tuple(new_edge)

        r, edge_r = lax.fori_loop(0, WSTEPS - 1, one_step, (wet, edge_wet))
        n = WSTEPS - 1
        sums = sweep(n, r, edge_r, True)
        for q in range(5):
            put(BANDS, sums[q], slice(8 * q, 8 * q + 8))
        swap = mesh_copy(BANDS, BANDR, t_send.at[n, 0], t_recv.at[n, 0], {"spec": other})
        swap.start()
        swap.wait_recv()
        full = [tuple(sums[q][h] + BANDR[8 * q : 8 * q + 8, halves[h]] for h in range(2)) for q in range(5)]
        breaking = tuple(1.0 / (1.0 + stiff[h] * full[0][h]) for h in range(2))
        final = tuple(wet[h] * breaking[h] for h in range(2))
        bands = []
        for q in range(1, 5):
            scale = breaking if q < 3 else final
            bands.append(circular(barrel(tuple(scale[h] * full[q][h] for h in range(2)), shift), 1))
        bands = [tuple(pltpu.roll(x, 32 * f, 1) if f else x for x in field) for f, field in enumerate(bands)]
        for u in range(TILES):
            MSG2[pl.ds(8 * u, 8), :] = windows(bands, u)

        def send_bands(u, carry):
            to_ocean(MSG2, BR, f_send, f_recv, u).start()
            return carry

        lax.fori_loop(0, TILES, send_bands, 0)

        def store(c):
            rows = pl.ds(pl.multiple_of(c * RCH * 8, 8), RCH * 8)
            return [
                pltpu.make_async_copy(B.at[h, rows, :], out_w.at[rows, hs], load_sem.at[c, h])
                for h, hs in enumerate(halves)
            ]

        def finish(c, carry):
            def scale_f(i, carry):
                for d in range(DLOC):
                    rows = pl.ds(pl.multiple_of((c * RCH + i * DLOC + d) * 8, 8), 8)
                    for h in range(2):
                        B[h, rows, :] = B[h, rows, :] * final[h]
                return carry

            lax.fori_loop(0, FCH, scale_f, 0)
            for copy in store(c):
                copy.start()
            return carry

        lax.fori_loop(0, CHUNKS, finish, 0)
        A2[...] = jnp.zeros((2, 192, 128), F32)
        blanks = [pltpu.make_async_copy(A2.at[h], out_o.at[:, hs], out_sem.at[h]) for h, hs in enumerate(halves)]
        for copy in blanks:
            copy.start()

        def drain(c, carry):
            for copy in store(c):
                copy.wait()

            @pl.when(has_hi)
            def _():
                for n in range(WSTEPS):
                    halo(n, 0, c).wait_send()

            @pl.when(has_lo)
            def _():
                for n in range(WSTEPS):
                    halo(n, 1, c).wait_send()

            return carry

        lax.fori_loop(0, CHUNKS, drain, 0)
        for copy in blanks:
            copy.wait()
        for m in range(WSTEPS - 1):
            for condition, copy in total_copies(m):
                gated(condition, copy.wait_send)
        swap.wait_send()
        gated(has_hi, neighbour(0).wait_send)
        gated(has_lo, neighbour(1).wait_send)
        settle(MMSG, m_send)
        settle(MSG2, f_send)

    @pl.when(grp == 1)
    def circulation():
        top = (1 - sp).astype(F32)
        deep = sp.astype(F32)
        down = jnp.where(sp == 0, 1.0, math.exp(-1.0)).astype(F32)
        loads = [
            pltpu.make_async_copy(ocean_h.at[:, halves[0]], Q.at[0], small_sem.at[0]),
            pltpu.make_async_copy(ocean_h.at[:, halves[1]], Q.at[1], small_sem.at[1]),
            pltpu.make_async_copy(sea_h, sea, small_sem.at[2]),
        ]
        for copy in loads:
            copy.start()
        for copy in loads:
            copy.wait()
        for c in range(2):
            for h, hs in enumerate(halves):
                acc = jnp.zeros((8, 128), F32)
                for k in range(KLOC):
                    acc += Q[h, pl.ds((c * KLOC + k) * 8, 8), :] * float(_wgt[k])
                CS[pl.ds(8 * c, 8), hs] = acc * down
        part = mesh_copy(CS, CR, c_send, c_recv, {"spec": other})
        part.start()

        def edge(n, side):
            return mesh_copy(
                ES.at[n, side], EH.at[n, side], e_send.at[n, side], e_recv.at[n, side],
                {"tile": hi_t if side == 0 else lo_t},
            )

        def level(n):
            return mesh_copy(LS.at[n], LH.at[n], l_send.at[n], l_recv.at[n], {"spec": other})

        def rims_out(n, src):
            for c in range(3):
                for h, hs in enumerate(halves):
                    ES[n, 0, pl.ds(8 * c, 8), hs] = src[h, pl.ds(c * 64 + 7, 8, stride=8), :]
                    ES[n, 1, pl.ds(8 * c, 8), hs] = src[h, pl.ds(c * 64, 8, stride=8), :]
                    LS[n, pl.ds(8 * c, 8), hs] = jnp.where(
                        sp == 0, src[h, pl.ds(c * 64 + 56, 8), :], src[h, pl.ds(c * 64, 8), :]
                    )
            pl.when(has_hi)(edge(n, 0).start)
            pl.when(has_lo)(edge(n, 1).start)
            level(n).start()

        SX[...] = jnp.zeros((128, 256), F32)
        put(SX, pair(sea), slice(16, 24))
        part.wait_recv()
        for c in range(2):
            rows = pl.ds(8 * c, 8)
            SX[rows, :] = CS[rows, :] + CR[rows, :]
        beside = (lane & 7) < 4
        for c in range(2):
            src = tuple(SX[pl.ds(8 + 8 * c, 8), hs] for hs in halves)
            ahead, behind = circular(src, 120), circular(src, 8)
            ahead = (ahead[1], ahead[0])
            put(SX, tuple(jnp.where(beside, ahead[h], behind[h]) for h in range(2)), slice(24 + 8 * c, 32 + 8 * c))
        for h, hs in enumerate(halves):
            MSG[pl.ds(128 * h, 128), :] = pltpu.roll(SX[:, hs].T, tile * 8 % 128, 1)

        def to_wave(u):
            return mesh_copy(
                MSG.at[pl.ds(pl.multiple_of(u * 8, 8), 8), :],
                QR.at[pl.ds(pl.multiple_of(tile * 8, 8), 8), :],
                q_send, q_recv, {"grp": 0, "tile": u},
            )

        def send_q(u, carry):
            to_wave(u).start()
            return carry

        lax.fori_loop(0, TILES, send_q, 0)
        rims_out(0, Q)

        zbuf[...] = jnp.zeros((RCH * 8, 256), F32)

        def blank(c):
            rows = pl.ds(pl.multiple_of(c * RCH * 8, 8), RCH * 8)
            return pltpu.make_async_copy(zbuf, out_w.at[rows, :], load_sem.at[c, 0])

        def begin(c, carry):
            blank(c).start()
            return carry

        lax.fori_loop(0, CHUNKS, begin, 0)

        @pl.when(jnp.logical_not(has_lo))
        def _():
            EH[:, 0] = jnp.zeros((2, 24, 256), F32)

        @pl.when(jnp.logical_not(has_hi))
        def _():
            EH[:, 1] = jnp.zeros((2, 24, 256), F32)

        at_lo = jnp.where(has_lo, 1.0, 0.0).astype(F32)
        at_hi = jnp.where(has_hi, 1.0, 0.0).astype(F32)

        def arrived(buf, slots):
            for h in range(2):
                turned = buf[pl.ds(128 * h, 128), :].T
                BTS[pl.ds(0, 128), halves[h]] = turned
                BTS[pl.ds(128, 128), halves[h]] = turned
            out = []
            for f in range(slots):
                start = pl.multiple_of((8 * tile + 32 * f) % 128, 8)
                wide = BTS[pl.ds(start, 16), :]
                out.append(tuple((wide[0:8, hs], wide[1:9, hs], wide[2:10, hs]) for hs in halves))
            return out

        settle(MR, m_recv)
        (mask3,) = arrived(MR, 1)
        mask = tuple(x[1] for x in mask3)
        mask_lo = tuple(jnp.where(first_row, x[0] * at_lo, x[0]) for x in mask3)
        mask_hi = tuple(jnp.where(last_row, x[2] * at_hi, x[2]) for x in mask3)

        def lateral(x, lower, upper):
            left, right = from_left(x), from_right(x)
            return tuple(lower[h] + upper[h] + left[h] + right[h] - 4.0 * x[h] for h in range(2))

        def substep(n, src, dst):
            for c in range(3):
                for k in range(KLOC):
                    at = (c * KLOC + k) * 8
                    x = tuple(src[h, pl.ds(at, 8), :] for h in range(2))
                    row_at = 8 * c + k
                    lower = tuple(
                        jnp.where(first_row, EH[n, 0, row_at : row_at + 1, hs], pltpu.roll(x[h], 1, 0))
                        for h, hs in enumerate(halves)
                    )
                    upper = tuple(
                        jnp.where(last_row, EH[n, 1, row_at : row_at + 1, hs], pltpu.roll(x[h], 7, 0))
                        for h, hs in enumerate(halves)
                    )
                    side = lateral(x, lower, upper)
                    for h, hs in enumerate(halves):
                        if k > 0:
                            above = src[h, pl.ds(at - 8, 8), :]
                        else:
                            above = LH[n, pl.ds(8 * c, 8), hs] * deep
                        if k < KLOC - 1:
                            below = src[h, pl.ds(at + 8, 8), :]
                        else:
                            below = LH[n, pl.ds(8 * c, 8), hs] * top
                        value = x[h] + 0.1 * side[h] + 0.2 * (above + below - 2.0 * x[h])
                        if c == 0:
                            value = value + 0.1 * src[h, pl.ds(at + 64, 8), :]
                        if c == 1:
                            value = value - 0.1 * src[h, pl.ds(at - 64, 8), :]
                        dst[h, pl.ds(at, 8), :] = value * mask[h]

        def rims_in(n):
            pl.when(has_lo)(edge(n, 0).wait_recv)
            pl.when(has_hi)(edge(n, 1).wait_recv)
            level(n).wait_recv()

        rims_in(0)
        substep(0, Q, A1)
        rims_out(1, A1)
        rims_in(1)
        substep(1, A1, A2)

        settle(BR, f_recv)
        forced, spread = [], []
        for f, three in enumerate(arrived(BR, 4)):
            lower = tuple(three[h][0] * mask_lo[h] for h in range(2))
            own = tuple(three[h][1] * mask[h] for h in range(2))
            upper = tuple(three[h][2] * mask_hi[h] for h in range(2))
            forced.append(own)
            spread.append(lateral(own, lower, upper))
        for k in range(KLOC):
            near, far = math.exp(0.125), math.exp(-0.125)
            prof = float(_prof[k]) * down
            above = near if k > 0 else near * deep
            below = far if k < KLOC - 1 else far * top
            stay = prof * (1.0 + 0.2 * (above + below - 2.0))
            for h, hs in enumerate(halves):
                east = (0.1 * prof) * forced[3][h]
                north = (-0.1 * prof) * forced[2][h]
                d_east = (0.1 * stay) * forced[3][h] + (0.01 * prof) * spread[3][h]
                d_north = (-0.1 * stay) * forced[2][h] - (0.01 * prof) * spread[2][h]
                if k == 0:
                    east = east + top * forced[0][h]
                    north = north + top * forced[1][h]
                    d_east = d_east + top * (0.6 * forced[0][h] + 0.1 * spread[0][h])
                    d_north = d_north + top * (0.6 * forced[1][h] + 0.1 * spread[1][h])
                if k == 1:
                    d_east = d_east + (0.2 * top) * forced[0][h]
                    d_north = d_north + (0.2 * top) * forced[1][h]
                A2[h, pl.ds(8 * k, 8), :] += mask[h] * (d_east + 0.1 * north) + east
                A2[h, pl.ds(64 + 8 * k, 8), :] += mask[h] * (d_north - 0.1 * east) + north
        results = [pltpu.make_async_copy(A2.at[h], out_o.at[:, hs], out_sem.at[h]) for h, hs in enumerate(halves)]
        for copy in results:
            copy.start()

        def drain(c, carry):
            blank(c).wait()
            return carry

        lax.fori_loop(0, CHUNKS, drain, 0)
        part.wait_send()
        for n in range(2):
            pl.when(has_hi)(edge(n, 0).wait_send)
            pl.when(has_lo)(edge(n, 1).wait_send)
            level(n).wait_send()
        settle(MSG, q_send)
        for copy in results:
            copy.wait()


def body(spectrum, wind, land_mask, intersection, ocean_state, sea_level):
    v = lambda *shape, dtype=F32: pltpu.VMEM(shape, dtype)
    dma = lambda *shape: pltpu.SemaphoreType.DMA(shape) if shape else pltpu.SemaphoreType.DMA
    anywhere = pl.BlockSpec(memory_space=pl.ANY)
    scratch = [
        v(2, FD * 8, 128), v(2, FD * 8, 128), v(DLOC, 8, 256), v(FD, 128),
        v(WSTEPS, 2, 2, FD, 128), v(WSTEPS, 2, 2, FD, 128),
        v(2, 8, 256), v(8, 256, dtype=jnp.int32), v(8, 256, dtype=jnp.int32),
        v(16, 256, dtype=jnp.int32), v(2, 16, 256, dtype=jnp.int32),
        v(256, 128), v(WSTEPS, 8, 256), v(WSTEPS, 5, 8, 256), v(40, 256), v(40, 256), v(256, 128), v(256, 128),
        v(2, 192, 128), v(2, 192, 128), v(2, 192, 128), v(8, 256), v(16, 256), v(16, 256), v(128, 256),
        v(256, 128), v(256, 128), v(256, 128), v(256, 256),
        v(2, 2, 24, 256), v(2, 2, 24, 256), v(2, 24, 256), v(2, 24, 256), v(RCH * 8, 256),
        dma(CHUNKS, 2), dma(3), dma(WSTEPS, 2, CHUNKS), dma(WSTEPS, 2, CHUNKS), dma(WSTEPS, 5), dma(WSTEPS, 5),
        dma(2), dma(2), dma(), dma(), dma(), dma(), dma(), dma(), dma(), dma(),
        dma(2, 2), dma(2, 2), dma(2), dma(2), dma(2),
    ]
    waves, ocean = pl.pallas_call(
        kernel,
        out_shape=(
            jax.ShapeDtypeStruct((FD * 8, 256), F32),
            jax.ShapeDtypeStruct((192, 256), F32),
        ),
        in_specs=[pl.BlockSpec(memory_space=pltpu.SMEM)] + [anywhere] * 6,
        out_specs=(anywhere, anywhere),
        scratch_shapes=scratch,
        compiler_params=pltpu.CompilerParams(has_side_effects=True, vmem_limit_bytes=48 << 20),
    )(
        jnp.asarray(TABLE),
        spectrum.reshape(FD * 8, 256),
        wind,
        land_mask,
        intersection,
        ocean_state.reshape(192, 256),
        sea_level.reshape(8, 256),
    )
    return waves.reshape(spectrum.shape), ocean.reshape(ocean_state.shape)


def solution(mesh):
    return jax.shard_map(
        body,
        mesh=mesh,
        in_specs=(
            P("grp", None, "spec", "tile", None),
            P(None, "tile", None),
            P("tile", None),
            P("tile", None),
            P("grp", None, "spec", "tile", None),
            P("grp", "tile", None),
        ),
        out_specs=(P("grp", None, "spec", "tile", None), P("grp", None, "spec", "tile", None)),
        check_vma=False,
    )
```

profile of v0, /device:TPU:65, one launch (start us, length us, event | category | flops | bytes accessed | tf_op | source)
XLA Modules:
  0.0 80.4 jit_solution(5710556627509782480)
XLA Ops:
  0.6 0.0 copy-start
  0.6 0.9 %copy-done = f32[1,3,8,8,256]{4,3,2,1,0:T(8,128)S(1)} copy-done((f32[1,3,8,8,256]{4,3,2,1,0:T(8,128)S(1)}, f32[1,3,8,8,256]{4,3,2,1,0:T(8,128)}, u32[]{:S(2)}) %copy-start) | copy-done | bytes 196632
  1.6 0.0 copy-start.1
  1.6 0.7 copy-done.1
  2.3 0.0 copy-start.2
  2.3 0.7 copy-done.2
  3.0 0.0 copy-start.3
  3.0 0.7 copy-done.3
  3.7 0.0 copy-start.4
  3.7 0.7 copy-done.4
  4.4 0.0 copy-start.5
  4.4 0.7 copy-done.5
  5.1 72.5 %shard_map.86 = (f32[4608,256]{1,0:T(8,128)S(1)}, f32[192,256]{1,0:T(8,128)S(1)}) custom-call(f32[5,32]{1,0:T(8,128)S(1)} %copy-done.5, f32[4608,256]{1,0:T(8,128)} %bitcast.9, f32[2,8,256]{2,1,0:T(8,128)S(1)} %copy-done.1, s32[8,256]{1,0:T(8,128)S(1)} %copy-done.2, s32[8,256]{1,0:T(8,128)S(1)} %copy-done.3, f32[192,256]{1,0:T(8,128)S(1)} %bitcast.6, ...), custom_call_target="tpu_custom_call" | custom-call | tf_op jit(solution)/shard_map/pallas_call | solution.py:695
  77.5 2.2 %copy.11 = f32[1,32,18,8,256]{4,3,2,1,0:T(8,128)} copy(f32[1,32,18,8,256]{4,3,2,1,0:T(8,128)S(1)} %bitcast.5) | data formatting | bytes 9437184
  79.7 0.7 copy.12
Async XLA Ops:
  0.6 0.9 %copy-start = (f32[1,3,8,8,256]{4,3,2,1,0:T(8,128)S(1)}, f32[1,3,8,8,256]{4,3,2,1,0:T(8,128)}, u32[]{:S(2)}) copy-start(f32[1,3,8,8,256]{4,3,2,1,0:T(8,128)} %param.11) | copy-start | bytes 589828
  1.6 0.7 copy-start.1
  2.3 0.7 copy-start.2
  3.0 0.7 copy-start.3
  3.7 0.7 copy-start.4
  4.4 0.7 copy-start.5
where the time goes:
time: 80.8 us; the launch traced here: 80.4 us
  Pallas kernels  72.5 us (90%)
  local copies, waits for them, and re-layouts  7.28 us (9%)
    pallas_call x1, Pallas kernels, body(): pl.pallas_call(kernel, out_shape=(jax.ShapeDtypeStruct((FD * 8, 256), F32...  72.5 us
    unnamed x14, local copies, waits for them, and re-layouts  7.28 us

commit v1 on v0

--- a/solution.py
+++ b/solution.py
@@ -29,6 +29,7 @@
 _ang = 2.0 * math.pi * (np.arange(DIRS) + 0.5) / DIRS
 COS = [float(np.float32(x)) for x in np.cos(_ang)[:DLOC]]
 SIN = [float(np.float32(x)) for x in np.sin(_ang)[:DLOC]]
+DIR_ORDER = [d for k in range(DLOC // 2) for d in (k, DLOC - 1 - k)]
 _prof = np.exp(-2.0 * (np.arange(LEVELS) + 0.5) / LEVELS)
 _wgt = _prof / _prof.sum()
 
@@ -49,8 +50,8 @@
 
 
 def kernel(
-    tab, spec_h, wind_h, land_h, inter_h, ocean_h, sea_h, out_w, out_o,
-    B, G, WD, CNT, H, S, wind, land, inter, NBS, NBR, QR, TS, TR, BANDS, BANDR, MSG2, MMSG,
+    spec_h, wind_h, land_h, inter_h, ocean_h, sea_h, out_w, out_o,
+    tab, B, G, WD, CNT, H, S, wind, land, inter, NBS, NBR, QR, TS, TR, BANDS, BANDR, MSG2, MMSG,
     Q, A1, A2, sea, CS, CR, SX, MSG, MR, BR, BTS, ES, EH, LS, LH, zbuf,
     load_sem, small_sem, h_send, h_recv, t_send, t_recv, nb_send, nb_recv,
     q_send, q_recv, m_send, m_recv, f_send, f_recv, c_send, c_recv, e_send, e_recv, l_send, l_recv, out_sem,
@@ -97,6 +98,33 @@
         for h in range(2):
             ref[rows, halves[h]] = value[h]
 
+    barrier = pltpu.get_barrier_semaphore()
+
+    def greet(where):
+        pl.semaphore_signal(barrier, 1, device_id=where, device_id_type=pl.DeviceIdType.MESH)
+
+    greet({"spec": other})
+
+    @pl.when(has_lo)
+    def _():
+        greet({"tile": lo_t})
+        greet({"tile": lo_t, "spec": other})
+
+    @pl.when(has_hi)
+    def _():
+        greet({"tile": hi_t})
+        greet({"tile": hi_t, "spec": other})
+
+    def greet_across(u, carry):
+        greet({"grp": 1 - grp, "tile": u})
+        return carry
+
+    lax.fori_loop(0, TILES, greet_across, 0)
+    beside = jnp.where(has_lo, 2, 0) + jnp.where(has_hi, 2, 0)
+
+    def everyone_in():
+        pl.semaphore_wait(barrier, TILES + 1 + beside)
+
     @pl.when(grp == 0)
     def wave():
         def load(c):
@@ -113,6 +141,9 @@
         ]
         for copy in smalls:
             copy.start()
+        for q in range(TABLE.shape[0]):
+            for f in range(FREQS):
+                tab[q, f] = float(TABLE[q, f])
 
         def begin(c, carry):
             for copy in load(c):
@@ -157,6 +188,8 @@
                 NBS, NBR.at[side], nb_send.at[side], nb_recv.at[side],
                 {"tile": hi_t if side == 0 else lo_t},
             )
+
+        everyone_in()
 
         @pl.when(has_hi)
         def _():
@@ -301,10 +334,10 @@
                 def band(fc, sums):
                     f = c * FCH + fc
                     sgs = tab[0, f] * sgn
-                    slope = tab[1, f]
                     zero = jnp.zeros((8, 128), F32)
                     acc = [[zero, zero] for _ in range(5 if last else 1)]
-                    for d in range(DLOC):
+                    half_way = {}
+                    for d in (DIR_ORDER if last else range(DLOC)):
                         i = f * DLOC + d
                         rows = pl.ds(pl.multiple_of(i * 8, 8), 8)
                         ce = sgs * COS[d]
@@ -332,11 +365,13 @@
                             B[h, rows, :] = new
                             acc[0][h] += adv
                             if last:
-                                push = adv * jnp.maximum(WD[d, :, hs] * slope - 0.05, 0.0)
-                                acc[1][h] += push * COS[d]
-                                acc[2][h] += push * SIN[d]
-                                acc[3][h] += new * COS[d]
-                                acc[4][h] += new * SIN[d]
+                                mine = (new - adv, new)
+                                if h not in half_way:
+                                    half_way[h] = mine
+                                    continue
+                                for q, (a, b) in enumerate(zip(half_way.pop(h), mine)):
+                                    acc[1 + 2 * q][h] += (a - b) * COS[DLOC - 1 - d]
+                                    acc[2 + 2 * q][h] += (a + b) * SIN[d]
                     weights = [tab[2, f], tab[3, f], tab[3, f], tab[4, f], tab[4, f]]
                     if last:
                         weights = weights[:1] + [w * sgn for w in weights[1:]]
@@ -487,6 +522,7 @@
                 for k in range(KLOC):
                     acc += Q[h, pl.ds((c * KLOC + k) * 8, 8), :] * float(_wgt[k])
                 CS[pl.ds(8 * c, 8), hs] = acc * down
+        everyone_in()
         part = mesh_copy(CS, CR, c_send, c_recv, {"spec": other})
         part.start()
 
@@ -517,12 +553,12 @@
         for c in range(2):
             rows = pl.ds(8 * c, 8)
             SX[rows, :] = CS[rows, :] + CR[rows, :]
-        beside = (lane & 7) < 4
+        ahead_rows = (lane & 7) < 4
         for c in range(2):
             src = tuple(SX[pl.ds(8 + 8 * c, 8), hs] for hs in halves)
             ahead, behind = circular(src, 120), circular(src, 8)
             ahead = (ahead[1], ahead[0])
-            put(SX, tuple(jnp.where(beside, ahead[h], behind[h]) for h in range(2)), slice(24 + 8 * c, 32 + 8 * c))
+            put(SX, tuple(jnp.where(ahead_rows, ahead[h], behind[h]) for h in range(2)), slice(24 + 8 * c, 32 + 8 * c))
         for h, hs in enumerate(halves):
             MSG[pl.ds(128 * h, 128), :] = pltpu.roll(SX[:, hs].T, tile * 8 % 128, 1)
 
@@ -678,8 +714,9 @@
 def body(spectrum, wind, land_mask, intersection, ocean_state, sea_level):
     v = lambda *shape, dtype=F32: pltpu.VMEM(shape, dtype)
     dma = lambda *shape: pltpu.SemaphoreType.DMA(shape) if shape else pltpu.SemaphoreType.DMA
-    anywhere = pl.BlockSpec(memory_space=pl.ANY)
+    anywhere = pl.BlockSpec(memory_space=pltpu.HBM)
     scratch = [
+        pltpu.SMEM(TABLE.shape, F32),
         v(2, FD * 8, 128), v(2, FD * 8, 128), v(DLOC, 8, 256), v(FD, 128),
         v(WSTEPS, 2, 2, FD, 128), v(WSTEPS, 2, 2, FD, 128),
         v(2, 8, 256), v(8, 256, dtype=jnp.int32), v(8, 256, dtype=jnp.int32),
@@ -698,18 +735,22 @@
             jax.ShapeDtypeStruct((FD * 8, 256), F32),
             jax.ShapeDtypeStruct((192, 256), F32),
         ),
-        in_specs=[pl.BlockSpec(memory_space=pltpu.SMEM)] + [anywhere] * 6,
+        in_specs=[anywhere] * 6,
         out_specs=(anywhere, anywhere),
         scratch_shapes=scratch,
-        compiler_params=pltpu.CompilerParams(has_side_effects=True, vmem_limit_bytes=48 << 20),
+        compiler_params=pltpu.CompilerParams(collective_id=0, has_side_effects=True, vmem_limit_bytes=48 << 20),
     )(
-        jnp.asarray(TABLE),
-        spectrum.reshape(FD * 8, 256),
-        wind,
-        land_mask,
-        intersection,
-        ocean_state.reshape(192, 256),
-        sea_level.reshape(8, 256),
+        *(
+            pltpu.with_memory_space_constraint(x, pltpu.HBM)
+            for x in (
+                spectrum.reshape(FD * 8, 256),
+                wind,
+                land_mask,
+                intersection,
+                ocean_state.reshape(192, 256),
+                sea_level.reshape(8, 256),
+            )
+        )
     )
     return waves.reshape(spectrum.shape), ocean.reshape(ocean_state.shape)
 

time: 80.8 us -> 69.6 us (0.86)
  Pallas kernels: 72.5 us -> 65.7 us
  local copies, waits for them, and re-layouts: 7.28 us -> 2.86 us
    pallas_call x1, Pallas kernels: 72.5 us -> 65.7 us  [body(): pl.pallas_call(kernel, out_shape=(jax.ShapeDtypeStruct((FD * 8, 256), F32...]
    unnamed x14 -> x2, local copies, waits for them, and re-layouts: 7.28 us -> 2.86 us
where the time goes in v1:
time: 69.6 us; the launch traced here: 69.2 us
  Pallas kernels  65.7 us (94%)
  local copies, waits for them, and re-layouts  2.86 us (4%)
    pallas_call x1, Pallas kernels, body(): pl.pallas_call(kernel, out_shape=(jax.ShapeDtypeStruct((FD * 8, 256), F32...  65.7 us
    unnamed x2, local copies, waits for them, and re-layouts  2.86 us

profile of v1, /device:TPU:65, one launch (start us, length us, event | category | flops | bytes accessed | tf_op | source)
XLA Modules:
  0.0 69.2 jit_solution(16663663155813032471)
XLA Ops:
  0.6 65.7 %shard_map.77 = (f32[4608,256]{1,0:T(8,128)S(1)}, f32[192,256]{1,0:T(8,128)S(1)}) custom-call(f32[4608,256]{1,0:T(8,128)} %bitcast.7, f32[2,8,256]{2,1,0:T(8,128)} %wind_h.1, s32[8,256]{1,0:T(8,128)} %land_h.1, s32[8,256]{1,0:T(8,128)} %inter_h.1, f32[192,256]{1,0:T(8,128)} %bitcast.8, f32[8,256]{1,0:T(8,128)} %bitcast.9), custom_call_target="tpu_custom_call" | custom-call | tf_op jit(solution)/shard_map/pallas_call | solution.py:732
  66.3 2.2 %copy.10 = f32[1,32,18,8,256]{4,3,2,1,0:T(8,128)} copy(f32[1,32,18,8,256]{4,3,2,1,0:T(8,128)S(1)} %bitcast.5) | data formatting | bytes 9437184
  68.5 0.7 copy.11

commit v2 on v1

--- a/solution.py
+++ b/solution.py
@@ -19,6 +19,7 @@
 CHUNKS = 8
 FCH = FREQS // CHUNKS
 RCH = FCH * DLOC
+PCH = 6
 F32 = jnp.float32
 
 _freq = 0.04 * 1.1 ** np.arange(FREQS)
@@ -51,7 +52,7 @@
 
 def kernel(
     spec_h, wind_h, land_h, inter_h, ocean_h, sea_h, out_w, out_o,
-    tab, B, G, WD, CNT, H, S, wind, land, inter, NBS, NBR, QR, TS, TR, BANDS, BANDR, MSG2, MMSG,
+    tab, B, G, PT, WD, CNT, H, S, wind, land, inter, NBS, NBR, QR, TS, TR, BANDS, BANDR, MSG2, MMSG,
     Q, A1, A2, sea, CS, CR, SX, MSG, MR, BR, BTS, ES, EH, LS, LH, zbuf,
     load_sem, small_sem, h_send, h_recv, t_send, t_recv, nb_send, nb_recv,
     q_send, q_recv, m_send, m_recv, f_send, f_recv, c_send, c_recv, e_send, e_recv, l_send, l_recv, out_sem,
@@ -311,25 +312,78 @@
         v_lo = tuple(jnp.broadcast_to(x[7:8], (8, 128)) for x in edge_v)
         v_hi = tuple(jnp.broadcast_to(x[0:1], (8, 128)) for x in edge_v)
 
+        def halo_in(n, c):
+            @pl.when(has_lo)
+            def _():
+                halo(n, 0, c).wait_recv()
+
+            @pl.when(has_hi)
+            def _():
+                halo(n, 1, c).wait_recv()
+
+            for k in range(RCH // 8):
+                rows = pl.ds(pl.multiple_of(c * RCH + 8 * k, 8), 8)
+                cn = CNT[rows, :]
+                for h in range(2):
+                    H[n, 0, h, rows, :] = jnp.maximum((cn + v_lo[h]) * H[n, 0, h, rows, :], 0.0)
+                    H[n, 1, h, rows, :] = jnp.minimum((cn + v_hi[h]) * H[n, 1, h, rows, :], 0.0)
+
+        def terms(n, i, rows, ce, cn):
+            b = [B[h, rows, :] for h in range(2)]
+            X = [(u01[h] + ce) * b[h] for h in range(2)]
+            Y = [(v01[h] + cn) * b[h] for h in range(2)]
+            own = [(b[h] - jnp.abs(X[h])) - jnp.abs(Y[h]) for h in range(2)]
+            a = [pltpu.roll(jnp.maximum(x, 0.0), 1, 1) for x in X]
+            west = [a[0], jnp.where(first_lane, a[0], a[1])]
+            a = [pltpu.roll(jnp.minimum(x, 0.0), 127, 1) for x in X]
+            east = [jnp.where(last_lane, a[1], a[0]), a[1]]
+            south = [
+                jnp.where(
+                    first_row, H[n, 0, h, pl.ds(i, 8, stride=0), :], pltpu.roll(jnp.maximum(Y[h], 0.0), 1, 0)
+                )
+                for h in range(2)
+            ]
+            north = [
+                jnp.where(
+                    last_row, H[n, 1, h, pl.ds(i, 8, stride=0), :], pltpu.roll(jnp.minimum(Y[h], 0.0), 7, 0)
+                )
+                for h in range(2)
+            ]
+            return own, west, east, south, north
+
+        def ahead(n):
+            def chunk(c, carry):
+                halo_in(n, c)
+
+                def band(fc, carry):
+                    f = c * FCH + fc
+                    sgs = tab[0, f] * sgn
+                    for d in range(DLOC):
+                        i = f * DLOC + d
+                        rows = pl.ds(pl.multiple_of(i * 8, 8), 8)
+                        for q, term in enumerate(terms(n, i, rows, sgs * COS[d], sgs * SIN[d])):
+                            for h in range(2):
+                                PT[q, h, rows, :] = term[h]
+                    return carry
+
+                return lax.fori_loop(0, FCH, band, carry)
+
+            lax.fori_loop(0, PCH, chunk, 0)
+
+        def factors(r, edge_r):
+            a, b = [pltpu.roll(x, 1, 1) for x in r], [pltpu.roll(x, 127, 1) for x in r]
+            r_w = (jnp.where(first_lane, 0.0, a[0]), jnp.where(first_lane, a[0], a[1]))
+            r_e = (jnp.where(last_lane, b[1], b[0]), jnp.where(last_lane, 0.0, b[1]))
+            r_s = tuple(jnp.where(first_row, pltpu.roll(edge_r[h], 1, 0), pltpu.roll(r[h], 1, 0)) for h in range(2))
+            r_n = tuple(jnp.where(last_row, pltpu.roll(edge_r[h], 7, 0), pltpu.roll(r[h], 7, 0)) for h in range(2))
+            return tuple(r), r_w, r_e, r_s, r_n
+
         def sweep(n, r, edge_r, last):
-            r_lo = tuple(jnp.broadcast_to(x[7:8], (8, 128)) for x in edge_r)
-            r_hi = tuple(jnp.broadcast_to(x[0:1], (8, 128)) for x in edge_r)
-
-            def chunk(c, sums):
-                @pl.when(has_lo)
-                def _():
-                    halo(n, 0, c).wait_recv()
-
-                @pl.when(has_hi)
-                def _():
-                    halo(n, 1, c).wait_recv()
-
-                for k in range(RCH // 8):
-                    rows = pl.ds(pl.multiple_of(c * RCH + 8 * k, 8), 8)
-                    cn = CNT[rows, :]
-                    for h in range(2):
-                        H[n, 0, h, rows, :] = jnp.maximum((cn + v_lo[h]) * (r_lo[h] * H[n, 0, h, rows, :]), 0.0)
-                        H[n, 1, h, rows, :] = jnp.minimum((cn + v_hi[h]) * (r_hi[h] * H[n, 1, h, rows, :]), 0.0)
+            r_all = factors(r, edge_r)
+
+            def chunk(c, sums, prepared):
+                if not prepared:
+                    halo_in(n, c)
 
                 def band(fc, sums):
                     f = c * FCH + fc
@@ -340,27 +394,13 @@
                     for d in (DIR_ORDER if last else range(DLOC)):
                         i = f * DLOC + d
                         rows = pl.ds(pl.multiple_of(i * 8, 8), 8)
-                        ce = sgs * COS[d]
-                        cn = sgs * SIN[d]
-                        E = [r[h] * B[h, rows, :] for h in range(2)]
-                        X = [(u01[h] + ce) * E[h] for h in range(2)]
-                        Y = [(v01[h] + cn) * E[h] for h in range(2)]
-                        west = from_left([jnp.maximum(x, 0.0) for x in X])
-                        east = from_right([jnp.minimum(x, 0.0) for x in X])
-                        for h, hs in enumerate(halves):
-                            south = jnp.where(
-                                first_row,
-                                H[n, 0, h, pl.ds(i, 8, stride=0), :],
-                                pltpu.roll(jnp.maximum(Y[h], 0.0), 1, 0),
-                            )
-                            north = jnp.where(
-                                last_row,
-                                H[n, 1, h, pl.ds(i, 8, stride=0), :],
-                                pltpu.roll(jnp.minimum(Y[h], 0.0), 7, 0),
-                            )
-                            adv = ((E[h] - jnp.abs(X[h])) - jnp.abs(Y[h])) + (
-                                (west[h] - east[h]) + (south - north)
-                            )
+                        if prepared:
+                            five = [[PT[q, h, rows, :] for h in range(2)] for q in range(5)]
+                        else:
+                            five = terms(n, i, rows, sgs * COS[d], sgs * SIN[d])
+                        for h in range(2):
+                            own, west, east, south, north = (r_all[q][h] * five[q][h] for q in range(5))
+                            adv = own + ((west - east) + (south - north))
                             new = adv * G[h, rows, :]
                             B[h, rows, :] = new
                             acc[0][h] += adv
@@ -381,12 +421,18 @@
 
                 sums = lax.fori_loop(0, FCH, band, sums)
                 if not last:
-                    edges_out(n + 1, c)
+
+                    @pl.when(c < CHUNKS - 1)
+                    def _():
+                        edges_out(n + 1, c)
+
                 return sums
 
             zero = jnp.zeros((8, 128), F32)
-            init = tuple((zero, zero) for _ in range(5 if last else 1))
-            return lax.fori_loop(0, CHUNKS, chunk, init)
+            sums = tuple((zero, zero) for _ in range(5 if last else 1))
+            begun = PCH if last else jnp.where(n > 0, PCH, 0)
+            sums = lax.fori_loop(0, begun, lambda c, x: chunk(c, x, True), sums)
+            return lax.fori_loop(begun, CHUNKS, lambda c, x: chunk(c, x, False), sums)
 
         def total_copies(n):
             return [
@@ -411,6 +457,8 @@
             copies = total_copies(n)
             for condition, copy in copies:
                 gated(condition, copy.start)
+            edges_out(n + 1, CHUNKS - 1)
+            ahead(n + 1)
             for (_, copy), condition in zip(copies, [None, has_lo, has_lo, has_hi, has_hi]):
                 gated(condition, copy.wait_recv)
             new_r, new_edge = [], []
@@ -717,7 +765,7 @@
     anywhere = pl.BlockSpec(memory_space=pltpu.HBM)
     scratch = [
         pltpu.SMEM(TABLE.shape, F32),
-        v(2, FD * 8, 128), v(2, FD * 8, 128), v(DLOC, 8, 256), v(FD, 128),
+        v(2, FD * 8, 128), v(2, FD * 8, 128), v(5, 2, PCH * RCH * 8, 128), v(DLOC, 8, 256), v(FD, 128),
         v(WSTEPS, 2, 2, FD, 128), v(WSTEPS, 2, 2, FD, 128),
         v(2, 8, 256), v(8, 256, dtype=jnp.int32), v(8, 256, dtype=jnp.int32),
         v(16, 256, dtype=jnp.int32), v(2, 16, 256, dtype=jnp.int32),

time: 69.6 us -> 64.7 us (0.930)
  Pallas kernels: 65.7 us -> 61.1 us
    pallas_call x1, Pallas kernels: 65.7 us -> 61.1 us  [body(): pl.pallas_call(kernel, out_shape=(jax.ShapeDtypeStruct((FD * 8, 256), F32...]
where the time goes in v2:
time: 64.7 us; the launch traced here: 64.6 us
  Pallas kernels  61.1 us (94%)
  local copies, waits for them, and re-layouts  2.86 us (4%)
    pallas_call x1, Pallas kernels, body(): pl.pallas_call(kernel, out_shape=(jax.ShapeDtypeStruct((FD * 8, 256), F32...  61.1 us
    unnamed x2, local copies, waits for them, and re-layouts  2.86 us

profile of v2, /device:TPU:65, one launch (start us, length us, event | category | flops | bytes accessed | tf_op | source)
XLA Modules:
  0.0 64.6 jit_solution(17725663796525832595)
XLA Ops:
  0.6 61.1 %shard_map.77 = (f32[4608,256]{1,0:T(8,128)S(1)}, f32[192,256]{1,0:T(8,128)S(1)}) custom-call(f32[4608,256]{1,0:T(8,128)} %bitcast.7, f32[2,8,256]{2,1,0:T(8,128)} %wind_h.1, s32[8,256]{1,0:T(8,128)} %land_h.1, s32[8,256]{1,0:T(8,128)} %inter_h.1, f32[192,256]{1,0:T(8,128)} %bitcast.8, f32[8,256]{1,0:T(8,128)} %bitcast.9), custom_call_target="tpu_custom_call" | custom-call | tf_op jit(solution)/shard_map/pallas_call | solution.py:780
  61.7 2.2 %copy.10 = f32[1,32,18,8,256]{4,3,2,1,0:T(8,128)} copy(f32[1,32,18,8,256]{4,3,2,1,0:T(8,128)S(1)} %bitcast.5) | data formatting | bytes 9437184
  63.9 0.7 %copy.11 = f32[1,3,8,8,256]{4,3,2,1,0:T(8,128)} copy(f32[1,3,8,8,256]{4,3,2,1,0:T(8,128)S(1)} %bitcast.6) | data formatting | bytes 393216

commit v3 on v2

--- a/solution.py
+++ b/solution.py
@@ -19,7 +19,8 @@
 CHUNKS = 8
 FCH = FREQS // CHUNKS
 RCH = FCH * DLOC
-PCH = 6
+PCH = 5
+HELD = 3
 F32 = jnp.float32
 
 _freq = 0.04 * 1.1 ** np.arange(FREQS)
@@ -312,7 +313,7 @@
         v_lo = tuple(jnp.broadcast_to(x[7:8], (8, 128)) for x in edge_v)
         v_hi = tuple(jnp.broadcast_to(x[0:1], (8, 128)) for x in edge_v)
 
-        def halo_in(n, c):
+        def halo_in(n, c, scale=None):
             @pl.when(has_lo)
             def _():
                 halo(n, 0, c).wait_recv()
@@ -325,18 +326,27 @@
                 rows = pl.ds(pl.multiple_of(c * RCH + 8 * k, 8), 8)
                 cn = CNT[rows, :]
                 for h in range(2):
-                    H[n, 0, h, rows, :] = jnp.maximum((cn + v_lo[h]) * H[n, 0, h, rows, :], 0.0)
-                    H[n, 1, h, rows, :] = jnp.minimum((cn + v_hi[h]) * H[n, 1, h, rows, :], 0.0)
-
-        def terms(n, i, rows, ce, cn):
+                    lower, upper = H[n, 0, h, rows, :], H[n, 1, h, rows, :]
+                    if scale is not None:
+                        lower, upper = scale[0][h] * lower, scale[1][h] * upper
+                    H[n, 0, h, rows, :] = jnp.maximum((cn + v_lo[h]) * lower, 0.0)
+                    H[n, 1, h, rows, :] = jnp.minimum((cn + v_hi[h]) * upper, 0.0)
+
+        def terms(n, i, rows, ce, cn, r=None):
             b = [B[h, rows, :] for h in range(2)]
+            if r is not None:
+                b = [r[h] * b[h] for h in range(2)]
             X = [(u01[h] + ce) * b[h] for h in range(2)]
             Y = [(v01[h] + cn) * b[h] for h in range(2)]
             own = [(b[h] - jnp.abs(X[h])) - jnp.abs(Y[h]) for h in range(2)]
-            a = [pltpu.roll(jnp.maximum(x, 0.0), 1, 1) for x in X]
-            west = [a[0], jnp.where(first_lane, a[0], a[1])]
-            a = [pltpu.roll(jnp.minimum(x, 0.0), 127, 1) for x in X]
-            east = [jnp.where(last_lane, a[1], a[0]), a[1]]
+            west, east = [jnp.maximum(x, 0.0) for x in X], [jnp.minimum(x, 0.0) for x in X]
+            if r is not None:
+                west, east = from_left(west), from_right(east)
+            else:
+                a = [pltpu.roll(x, 1, 1) for x in west]
+                west = [a[0], jnp.where(first_lane, a[0], a[1])]
+                a = [pltpu.roll(x, 127, 1) for x in east]
+                east = [jnp.where(last_lane, a[1], a[0]), a[1]]
             south = [
                 jnp.where(
                     first_row, H[n, 0, h, pl.ds(i, 8, stride=0), :], pltpu.roll(jnp.maximum(Y[h], 0.0), 1, 0)
@@ -380,10 +390,14 @@
 
         def sweep(n, r, edge_r, last):
             r_all = factors(r, edge_r)
+            scale = (
+                tuple(jnp.broadcast_to(x[7:8], (8, 128)) for x in edge_r),
+                tuple(jnp.broadcast_to(x[0:1], (8, 128)) for x in edge_r),
+            )
 
             def chunk(c, sums, prepared):
                 if not prepared:
-                    halo_in(n, c)
+                    halo_in(n, c, scale)
 
                 def band(fc, sums):
                     f = c * FCH + fc
@@ -395,11 +409,11 @@
                         i = f * DLOC + d
                         rows = pl.ds(pl.multiple_of(i * 8, 8), 8)
                         if prepared:
-                            five = [[PT[q, h, rows, :] for h in range(2)] for q in range(5)]
+                            five = [[r_all[q][h] * PT[q, h, rows, :] for h in range(2)] for q in range(5)]
                         else:
-                            five = terms(n, i, rows, sgs * COS[d], sgs * SIN[d])
+                            five = terms(n, i, rows, sgs * COS[d], sgs * SIN[d], r)
                         for h in range(2):
-                            own, west, east, south, north = (r_all[q][h] * five[q][h] for q in range(5))
+                            own, west, east, south, north = (five[q][h] for q in range(5))
                             adv = own + ((west - east) + (south - north))
                             new = adv * G[h, rows, :]
                             B[h, rows, :] = new
@@ -422,7 +436,7 @@
                 sums = lax.fori_loop(0, FCH, band, sums)
                 if not last:
 
-                    @pl.when(c < CHUNKS - 1)
+                    @pl.when(c < CHUNKS - HELD)
                     def _():
                         edges_out(n + 1, c)
 
@@ -457,7 +471,12 @@
             copies = total_copies(n)
             for condition, copy in copies:
                 gated(condition, copy.start)
-            edges_out(n + 1, CHUNKS - 1)
+
+            def late(c, carry):
+                edges_out(n + 1, c)
+                return carry
+
+            lax.fori_loop(CHUNKS - HELD, CHUNKS, late, 0)
             ahead(n + 1)
             for (_, copy), condition in zip(copies, [None, has_lo, has_lo, has_hi, has_hi]):
                 gated(condition, copy.wait_recv)

time: 64.7 us -> 61 us (0.943)
  Pallas kernels: 61.1 us -> 57.3 us
    pallas_call x1, Pallas kernels: 61.1 us -> 57.3 us  [body(): pl.pallas_call(kernel, out_shape=(jax.ShapeDtypeStruct((FD * 8, 256), F32...]
where the time goes in v3:
time: 61 us; the launch traced here: 60.8 us
  Pallas kernels  57.3 us (94%)
  local copies, waits for them, and re-layouts  2.86 us (5%)
  between operations  0.64 us (1%)
    pallas_call x1, Pallas kernels, body(): pl.pallas_call(kernel, out_shape=(jax.ShapeDtypeStruct((FD * 8, 256), F32...  57.3 us
    unnamed x2, local copies, waits for them, and re-layouts  2.86 us

profile of v3, /device:TPU:65, one launch (start us, length us, event | category | flops | bytes accessed | tf_op | source)
XLA Modules:
  0.0 60.8 jit_solution(13988442232655680119)
XLA Ops:
  0.6 57.3 %shard_map.77 = (f32[4608,256]{1,0:T(8,128)S(1)}, f32[192,256]{1,0:T(8,128)S(1)}) custom-call(f32[4608,256]{1,0:T(8,128)} %bitcast.7, f32[2,8,256]{2,1,0:T(8,128)} %wind_h.1, s32[8,256]{1,0:T(8,128)} %land_h.1, s32[8,256]{1,0:T(8,128)} %inter_h.1, f32[192,256]{1,0:T(8,128)} %bitcast.8, f32[8,256]{1,0:T(8,128)} %bitcast.9), custom_call_target="tpu_custom_call" | custom-call | tf_op jit(solution)/shard_map/pallas_call | solution.py:799
  57.9 2.2 %copy.10 = f32[1,32,18,8,256]{4,3,2,1,0:T(8,128)} copy(f32[1,32,18,8,256]{4,3,2,1,0:T(8,128)S(1)} %bitcast.5) | data formatting | bytes 9437184
  60.1 0.7 %copy.11 = f32[1,3,8,8,256]{4,3,2,1,0:T(8,128)} copy(f32[1,3,8,8,256]{4,3,2,1,0:T(8,128)S(1)} %bitcast.6) | data formatting | bytes 393216

commit v4 on v3

--- a/solution.py
+++ b/solution.py
@@ -51,10 +51,45 @@
     pltpu.make_async_copy(buf, buf, sem).wait()
 
 
+HALVES = (slice(0, 128), slice(128, 256))
+
+
+def at_lane(k):
+    return lax.broadcasted_iota(jnp.int32, (8, 128), 1) == k
+
+
+def from_left(x):
+    a, b = pltpu.roll(x[0], 1, 1), pltpu.roll(x[1], 1, 1)
+    return jnp.where(at_lane(0), 0.0, a), jnp.where(at_lane(0), a, b)
+
+
+def from_right(x):
+    a, b = pltpu.roll(x[0], 127, 1), pltpu.roll(x[1], 127, 1)
+    return jnp.where(at_lane(127), b, a), jnp.where(at_lane(127), 0.0, b)
+
+
+def lateral(x, lower, upper):
+    left, right = from_left(x), from_right(x)
+    return tuple(lower[h] + upper[h] + left[h] + right[h] - 4.0 * x[h] for h in range(2))
+
+
+def arrived(buf, BTS, tile, slots):
+    for h in range(2):
+        turned = buf[pl.ds(128 * h, 128), :].T
+        BTS[pl.ds(0, 128), HALVES[h]] = turned
+        BTS[pl.ds(128, 128), HALVES[h]] = turned
+    out = []
+    for f in range(slots):
+        start = pl.multiple_of((8 * tile + 32 * f) % 128, 8)
+        wide = BTS[pl.ds(start, 16), :]
+        out.append(tuple((wide[0:8, hs], wide[1:9, hs], wide[2:10, hs]) for hs in HALVES))
+    return out
+
+
 def kernel(
-    spec_h, wind_h, land_h, inter_h, ocean_h, sea_h, out_w, out_o,
+    spec_h, wind_h, land_h, inter_h, ocean_h, sea_h, out_w, out_o, BR, out_m,
     tab, B, G, PT, WD, CNT, H, S, wind, land, inter, NBS, NBR, QR, TS, TR, BANDS, BANDR, MSG2, MMSG,
-    Q, A1, A2, sea, CS, CR, SX, MSG, MR, BR, BTS, ES, EH, LS, LH, zbuf,
+    Q, A1, A2, sea, CS, CR, SX, MSG, MR, BTS, ES, EH, LS, LH,
     load_sem, small_sem, h_send, h_recv, t_send, t_recv, nb_send, nb_recv,
     q_send, q_recv, m_send, m_recv, f_send, f_recv, c_send, c_recv, e_send, e_recv, l_send, l_recv, out_sem,
 ):
@@ -72,15 +107,7 @@
     first_lane, last_lane = lane == 0, lane == 127
     first_row, last_row = row == 0, row == 7
     low_rows = row < 4
-    halves = (slice(0, 128), slice(128, 256))
-
-    def from_left(x):
-        a, b = pltpu.roll(x[0], 1, 1), pltpu.roll(x[1], 1, 1)
-        return jnp.where(first_lane, 0.0, a), jnp.where(first_lane, a, b)
-
-    def from_right(x):
-        a, b = pltpu.roll(x[0], 127, 1), pltpu.roll(x[1], 127, 1)
-        return jnp.where(last_lane, b, a), jnp.where(last_lane, 0.0, b)
+    halves = HALVES
 
     def circular(x, shift):
         a, b = pltpu.roll(x[0], shift, 1), pltpu.roll(x[1], shift, 1)
@@ -376,7 +403,7 @@
                                 PT[q, h, rows, :] = term[h]
                     return carry
 
-                return lax.fori_loop(0, FCH, band, carry)
+                return lax.fori_loop(0, FCH, band, carry, unroll=2)
 
             lax.fori_loop(0, PCH, chunk, 0)
 
@@ -433,7 +460,7 @@
                         tuple(total[h] + acc[q][h] * weights[q] for h in range(2)) for q, total in enumerate(sums)
                     )
 
-                sums = lax.fori_loop(0, FCH, band, sums)
+                sums = lax.fori_loop(0, FCH, band, sums, unroll=2)
                 if not last:
 
                     @pl.when(c < CHUNKS - HELD)
@@ -536,11 +563,6 @@
             return carry
 
         lax.fori_loop(0, CHUNKS, finish, 0)
-        A2[...] = jnp.zeros((2, 192, 128), F32)
-        blanks = [pltpu.make_async_copy(A2.at[h], out_o.at[:, hs], out_sem.at[h]) for h, hs in enumerate(halves)]
-        for copy in blanks:
-            copy.start()
-
         def drain(c, carry):
             for copy in store(c):
                 copy.wait()
@@ -558,8 +580,6 @@
             return carry
 
         lax.fori_loop(0, CHUNKS, drain, 0)
-        for copy in blanks:
-            copy.wait()
         for m in range(WSTEPS - 1):
             for condition, copy in total_copies(m):
                 gated(condition, copy.wait_send)
@@ -643,18 +663,6 @@
         lax.fori_loop(0, TILES, send_q, 0)
         rims_out(0, Q)
 
-        zbuf[...] = jnp.zeros((RCH * 8, 256), F32)
-
-        def blank(c):
-            rows = pl.ds(pl.multiple_of(c * RCH * 8, 8), RCH * 8)
-            return pltpu.make_async_copy(zbuf, out_w.at[rows, :], load_sem.at[c, 0])
-
-        def begin(c, carry):
-            blank(c).start()
-            return carry
-
-        lax.fori_loop(0, CHUNKS, begin, 0)
-
         @pl.when(jnp.logical_not(has_lo))
         def _():
             EH[:, 0] = jnp.zeros((2, 24, 256), F32)
@@ -663,30 +671,11 @@
         def _():
             EH[:, 1] = jnp.zeros((2, 24, 256), F32)
 
-        at_lo = jnp.where(has_lo, 1.0, 0.0).astype(F32)
-        at_hi = jnp.where(has_hi, 1.0, 0.0).astype(F32)
-
-        def arrived(buf, slots):
-            for h in range(2):
-                turned = buf[pl.ds(128 * h, 128), :].T
-                BTS[pl.ds(0, 128), halves[h]] = turned
-                BTS[pl.ds(128, 128), halves[h]] = turned
-            out = []
-            for f in range(slots):
-                start = pl.multiple_of((8 * tile + 32 * f) % 128, 8)
-                wide = BTS[pl.ds(start, 16), :]
-                out.append(tuple((wide[0:8, hs], wide[1:9, hs], wide[2:10, hs]) for hs in halves))
-            return out
-
         settle(MR, m_recv)
-        (mask3,) = arrived(MR, 1)
+        flags = pltpu.make_async_copy(MR, out_m, small_sem.at[0])
+        flags.start()
+        (mask3,) = arrived(MR, BTS, tile, 1)
         mask = tuple(x[1] for x in mask3)
-        mask_lo = tuple(jnp.where(first_row, x[0] * at_lo, x[0]) for x in mask3)
-        mask_hi = tuple(jnp.where(last_row, x[2] * at_hi, x[2]) for x in mask3)
-
-        def lateral(x, lower, upper):
-            left, right = from_left(x), from_right(x)
-            return tuple(lower[h] + upper[h] + left[h] + right[h] - 4.0 * x[h] for h in range(2))
 
         def substep(n, src, dst):
             for c in range(3):
@@ -730,9 +719,68 @@
         rims_in(1)
         substep(1, A1, A2)
 
+        results = [pltpu.make_async_copy(A2.at[h], out_o.at[:, hs], out_sem.at[h]) for h, hs in enumerate(halves)]
+        for copy in results:
+            copy.start()
+        part.wait_send()
+        for n in range(2):
+            pl.when(has_hi)(edge(n, 0).wait_send)
+            pl.when(has_lo)(edge(n, 1).wait_send)
+            level(n).wait_send()
+        settle(MSG, q_send)
+        flags.wait()
+        for copy in results:
+            copy.wait()
         settle(BR, f_recv)
+
+
+def tail(wave_h, unforced_h, bands_h, flags_h, out_w, out_o, zeros, A2, BR, MR, BTS, in_sem, w_sem, o_sem):
+    grp = lax.axis_index("grp")
+    tile = lax.axis_index("tile")
+    sp = lax.axis_index("spec")
+
+    @pl.when(grp == 0)
+    def wave():
+        copies = []
+        for c in range(CHUNKS):
+            rows = pl.ds(c * RCH * 8, RCH * 8)
+            copies.append(pltpu.make_async_copy(wave_h.at[rows, :], out_w.at[rows, :], w_sem.at[c]))
+            copies[-1].start()
+        zeros[0:192, :] = jnp.zeros((192, 256), F32)
+        copies.append(pltpu.make_async_copy(zeros.at[0:192, :], out_o, o_sem.at[0]))
+        copies[-1].start()
+        for copy in copies:
+            copy.wait()
+
+    @pl.when(grp == 1)
+    def circulation():
+        loads = [
+            pltpu.make_async_copy(flags_h, MR, in_sem.at[0]),
+            pltpu.make_async_copy(bands_h, BR, in_sem.at[1]),
+        ] + [pltpu.make_async_copy(unforced_h.at[:, hs], A2.at[h], in_sem.at[2 + h]) for h, hs in enumerate(HALVES)]
+        for copy in loads:
+            copy.start()
+        zeros[...] = jnp.zeros(zeros.shape, F32)
+        blanks = []
+        for c in range(CHUNKS):
+            rows = pl.ds(c * RCH * 8, RCH * 8)
+            blanks.append(pltpu.make_async_copy(zeros, out_w.at[rows, :], w_sem.at[c]))
+            blanks[-1].start()
+        row = lax.broadcasted_iota(jnp.int32, (8, 128), 0)
+        top = (1 - sp).astype(F32)
+        deep = sp.astype(F32)
+        down = jnp.where(sp == 0, 1.0, math.exp(-1.0)).astype(F32)
+        at_lo = jnp.where(tile > 0, 1.0, 0.0).astype(F32)
+        at_hi = jnp.where(tile < TILES - 1, 1.0, 0.0).astype(F32)
+        loads[0].wait()
+        (mask3,) = arrived(MR, BTS, tile, 1)
+        mask = tuple(x[1] for x in mask3)
+        mask_lo = tuple(jnp.where(row == 0, x[0] * at_lo, x[0]) for x in mask3)
+        mask_hi = tuple(jnp.where(row == 7, x[2] * at_hi, x[2]) for x in mask3)
+        for copy in loads[1:]:
+            copy.wait()
         forced, spread = [], []
-        for f, three in enumerate(arrived(BR, 4)):
+        for f, three in enumerate(arrived(BR, BTS, tile, 4)):
             lower = tuple(three[h][0] * mask_lo[h] for h in range(2))
             own = tuple(three[h][1] * mask[h] for h in range(2))
             upper = tuple(three[h][2] * mask_hi[h] for h in range(2))
@@ -744,7 +792,7 @@
             above = near if k > 0 else near * deep
             below = far if k < KLOC - 1 else far * top
             stay = prof * (1.0 + 0.2 * (above + below - 2.0))
-            for h, hs in enumerate(halves):
+            for h, hs in enumerate(HALVES):
                 east = (0.1 * prof) * forced[3][h]
                 north = (-0.1 * prof) * forced[2][h]
                 d_east = (0.1 * stay) * forced[3][h] + (0.01 * prof) * spread[3][h]
@@ -759,22 +807,11 @@
                     d_north = d_north + (0.2 * top) * forced[1][h]
                 A2[h, pl.ds(8 * k, 8), :] += mask[h] * (d_east + 0.1 * north) + east
                 A2[h, pl.ds(64 + 8 * k, 8), :] += mask[h] * (d_north - 0.1 * east) + north
-        results = [pltpu.make_async_copy(A2.at[h], out_o.at[:, hs], out_sem.at[h]) for h, hs in enumerate(halves)]
+        results = [pltpu.make_async_copy(A2.at[h], out_o.at[:, hs], o_sem.at[h]) for h, hs in enumerate(HALVES)]
         for copy in results:
             copy.start()
 
-        def drain(c, carry):
-            blank(c).wait()
-            return carry
-
-        lax.fori_loop(0, CHUNKS, drain, 0)
-        part.wait_send()
-        for n in range(2):
-            pl.when(has_hi)(edge(n, 0).wait_send)
-            pl.when(has_lo)(edge(n, 1).wait_send)
-            level(n).wait_send()
-        settle(MSG, q_send)
-        for copy in results:
+        for copy in results + blanks:
             copy.wait()
 
 
@@ -790,20 +827,22 @@
         v(16, 256, dtype=jnp.int32), v(2, 16, 256, dtype=jnp.int32),
         v(256, 128), v(WSTEPS, 8, 256), v(WSTEPS, 5, 8, 256), v(40, 256), v(40, 256), v(256, 128), v(256, 128),
         v(2, 192, 128), v(2, 192, 128), v(2, 192, 128), v(8, 256), v(16, 256), v(16, 256), v(128, 256),
-        v(256, 128), v(256, 128), v(256, 128), v(256, 256),
-        v(2, 2, 24, 256), v(2, 2, 24, 256), v(2, 24, 256), v(2, 24, 256), v(RCH * 8, 256),
+        v(256, 128), v(256, 128), v(256, 256),
+        v(2, 2, 24, 256), v(2, 2, 24, 256), v(2, 24, 256), v(2, 24, 256),
         dma(CHUNKS, 2), dma(3), dma(WSTEPS, 2, CHUNKS), dma(WSTEPS, 2, CHUNKS), dma(WSTEPS, 5), dma(WSTEPS, 5),
         dma(2), dma(2), dma(), dma(), dma(), dma(), dma(), dma(), dma(), dma(),
         dma(2, 2), dma(2, 2), dma(2), dma(2), dma(2),
     ]
-    waves, ocean = pl.pallas_call(
+    landed = pl.pallas_call(
         kernel,
         out_shape=(
             jax.ShapeDtypeStruct((FD * 8, 256), F32),
             jax.ShapeDtypeStruct((192, 256), F32),
+            jax.ShapeDtypeStruct((256, 128), F32),
+            jax.ShapeDtypeStruct((256, 128), F32),
         ),
         in_specs=[anywhere] * 6,
-        out_specs=(anywhere, anywhere),
+        out_specs=(pl.BlockSpec(memory_space=pl.ANY),) * 4,
         scratch_shapes=scratch,
         compiler_params=pltpu.CompilerParams(collective_id=0, has_side_effects=True, vmem_limit_bytes=48 << 20),
     )(
@@ -819,6 +858,16 @@
             )
         )
     )
+    waves, ocean = pl.pallas_call(
+        tail,
+        out_shape=(jax.ShapeDtypeStruct((FD * 8, 256), F32), jax.ShapeDtypeStruct((192, 256), F32)),
+        in_specs=[pl.BlockSpec(memory_space=pl.ANY)] * 4,
+        out_specs=(pl.BlockSpec(memory_space=pl.ANY),) * 2,
+        scratch_shapes=[
+            v(RCH * 8, 256), v(2, 192, 128), v(256, 128), v(256, 128), v(256, 256), dma(4), dma(CHUNKS), dma(2)
+        ],
+        compiler_params=pltpu.CompilerParams(vmem_limit_bytes=6 << 20),
+    )(*landed)
     return waves.reshape(spectrum.shape), ocean.reshape(ocean_state.shape)
 
 

time: 61 us -> 59.3 us (0.972)
  local copies, waits for them, and re-layouts: 2.86 us -> 0 us
  Pallas kernels: 57.3 us -> 58.3 us
    unnamed x2 -> x0, local copies, waits for them, and re-layouts: 2.86 us -> none
    pallas_call x0 -> x1, Pallas kernels: none -> 2.77 us  [body(): pl.pallas_call(tail, out_shape=(jax.ShapeDtypeStruct((FD * 8, 256), F32),...]
    pallas_call x1, Pallas kernels: 57.3 us -> 55.5 us  [body(): pl.pallas_call(kernel, out_shape=(jax.ShapeDtypeStruct((FD * 8, 256), F32...]
where the time goes in v4:
time: 59.3 us; the launch traced here: 58.9 us
  Pallas kernels  58.3 us (98%)
  between operations  0.64 us (1%)
    pallas_call x1, Pallas kernels, body(): pl.pallas_call(kernel, out_shape=(jax.ShapeDtypeStruct((FD * 8, 256), F32...  55.5 us
    pallas_call x1, Pallas kernels, body(): pl.pallas_call(tail, out_shape=(jax.ShapeDtypeStruct((FD * 8, 256), F32),...  2.77 us

profile of v4, /device:TPU:65, one launch (start us, length us, event | category | flops | bytes accessed | tf_op | source)
XLA Modules:
  0.0 58.9 jit_solution(2639877296320419866)
XLA Ops:
  0.6 55.5 %shard_map.77 = (f32[4608,256]{1,0:T(8,128)S(1)}, f32[192,256]{1,0:T(8,128)S(1)}, f32[256,128]{1,0:T(8,128)S(1)}, f32[256,128]{1,0:T(8,128)S(1)}) custom-call(f32[4608,256]{1,0:T(8,128)} %bitcast.5, f32[2,8,256]{2,1,0:T(8,128)} %wind_h.1, s32[8,256]{1,0:T(8,128)} %land_h.1, s32[8,256]{1,0:T(8,128)} %inter_h.1, f32[192,256]{1,0:T(8,128)} %bitcast.6, ...), custom_call_target="tpu_custom_call" | custom-call | tf_op jit(solution)/shard_map/pallas_call | solution.py:836
  56.1 2.8 %shard_map.78 = (f32[4608,256]{1,0:T(8,128)}, f32[192,256]{1,0:T(8,128)}) custom-call(f32[4608,256]{1,0:T(8,128)S(1)} %get-tuple-element.8.wave_h, f32[192,256]{1,0:T(8,128)S(1)} %get-tuple-element.9.unforced_h, f32[256,128]{1,0:T(8,128)S(1)} %get-tuple-element.10.bands_h, f32[256,128]{1,0:T(8,128)S(1)} %get-tuple-element.11.flags_h), custom_call_target="tpu_custom_call" | custom-call | tf_op jit(solution)/shard_map/pallas_call | solution.py:861

commit v5 on v4

--- a/solution.py
+++ b/solution.py
@@ -89,9 +89,9 @@
 def kernel(
     spec_h, wind_h, land_h, inter_h, ocean_h, sea_h, out_w, out_o, BR, out_m,
     tab, B, G, PT, WD, CNT, H, S, wind, land, inter, NBS, NBR, QR, TS, TR, BANDS, BANDR, MSG2, MMSG,
-    Q, A1, A2, sea, CS, CR, SX, MSG, MR, BTS, ES, EH, LS, LH,
+    Q, A1, A2, sea, CS, SX, MSG, MR, BTS, ES, EH, LS, LH,
     load_sem, small_sem, h_send, h_recv, t_send, t_recv, nb_send, nb_recv,
-    q_send, q_recv, m_send, m_recv, f_send, f_recv, c_send, c_recv, e_send, e_recv, l_send, l_recv, out_sem,
+    q_send, q_recv, m_send, m_recv, f_send, f_recv, e_send, e_recv, l_send, l_recv, out_sem,
 ):
     grp = lax.axis_index("grp")
     tile = lax.axis_index("tile")
@@ -146,13 +146,14 @@
 
     def greet_across(u, carry):
         greet({"grp": 1 - grp, "tile": u})
+        greet({"grp": 1 - grp, "tile": u, "spec": other})
         return carry
 
     lax.fori_loop(0, TILES, greet_across, 0)
     beside = jnp.where(has_lo, 2, 0) + jnp.where(has_hi, 2, 0)
 
     def everyone_in():
-        pl.semaphore_wait(barrier, TILES + 1 + beside)
+        pl.semaphore_wait(barrier, 2 * TILES + 1 + beside)
 
     @pl.when(grp == 0)
     def wave():
@@ -315,16 +316,23 @@
         )
 
         settle(QR, q_recv)
-        fields = []
-        for c in range(5):
-            parts = []
-            for h in range(2):
-                acc = jnp.zeros((8, 128), F32)
-                for k in range(16):
-                    u = 16 * h + k
-                    acc = jnp.where((lane >> 3) == (k + c) % 16, QR[pl.ds(8 * u, 8), :], acc)
-                parts.append(pltpu.roll(acc, 128 - 8 * c, 1) if c else acc)
-            fields.append(tuple(parts))
+        group = lax.broadcasted_iota(jnp.int32, (4, 128), 1) >> 3
+        parts = [[], [], [], [], []]
+        for h in range(2):
+            upper = [jnp.zeros((4, 128), F32)] * 5
+            lower = [jnp.zeros((4, 128), F32)] * 5
+            for k in range(16):
+                m = QR[0, 16 * h + k] + QR[1, 16 * h + k]
+                turned = pltpu.roll(m, 64, 1)
+                for c in range(5):
+                    at = (k + c) % 16
+                    near, far = (m, turned) if at < 8 else (turned, m)
+                    upper[c] = jnp.where(group == at, near, upper[c])
+                    lower[c] = jnp.where(group == at, far, lower[c])
+            for c in range(5):
+                acc = jnp.concatenate([upper[c], lower[c]], axis=0)
+                parts[c].append(pltpu.roll(acc, 128 - 8 * c, 1) if c else acc)
+        fields = [tuple(x) for x in parts]
         left = tuple((256 - x) & 255 for x in shift)
         edge_left = tuple((256 - x) & 255 for x in edge_shift)
         u01 = tuple(0.1 * x for x in barrel(fields[0], left))
@@ -609,9 +617,6 @@
                 for k in range(KLOC):
                     acc += Q[h, pl.ds((c * KLOC + k) * 8, 8), :] * float(_wgt[k])
                 CS[pl.ds(8 * c, 8), hs] = acc * down
-        everyone_in()
-        part = mesh_copy(CS, CR, c_send, c_recv, {"spec": other})
-        part.start()
 
         def edge(n, side):
             return mesh_copy(
@@ -635,29 +640,30 @@
             level(n).start()
 
         SX[...] = jnp.zeros((128, 256), F32)
-        put(SX, pair(sea), slice(16, 24))
-        part.wait_recv()
-        for c in range(2):
-            rows = pl.ds(8 * c, 8)
-            SX[rows, :] = CS[rows, :] + CR[rows, :]
+        put(SX, tuple(0.5 * x for x in pair(sea)), slice(16, 24))
+        SX[0:16, :] = CS[...]
         ahead_rows = (lane & 7) < 4
         for c in range(2):
             src = tuple(SX[pl.ds(8 + 8 * c, 8), hs] for hs in halves)
             ahead, behind = circular(src, 120), circular(src, 8)
             ahead = (ahead[1], ahead[0])
             put(SX, tuple(jnp.where(ahead_rows, ahead[h], behind[h]) for h in range(2)), slice(24 + 8 * c, 32 + 8 * c))
+        slot = lax.broadcasted_iota(jnp.int32, (4, 128), 1) < 64
         for h, hs in enumerate(halves):
-            MSG[pl.ds(128 * h, 128), :] = pltpu.roll(SX[:, hs].T, tile * 8 % 128, 1)
-
-        def to_wave(u):
+            turned = pltpu.roll(SX[:, hs].T, tile % 8 * 8, 1)
+            turned = turned + pltpu.roll(turned, 64, 1)
+            for k in range(16):
+                MSG[16 * h + k] = jnp.where(slot, turned[8 * k : 8 * k + 4], turned[8 * k + 4 : 8 * k + 8])
+        everyone_in()
+
+        def to_wave(u, half):
             return mesh_copy(
-                MSG.at[pl.ds(pl.multiple_of(u * 8, 8), 8), :],
-                QR.at[pl.ds(pl.multiple_of(tile * 8, 8), 8), :],
-                q_send, q_recv, {"grp": 0, "tile": u},
+                MSG.at[u], QR.at[sp, tile], q_send, q_recv, {"grp": 0, "tile": u, "spec": half},
             )
 
         def send_q(u, carry):
-            to_wave(u).start()
+            to_wave(u, sp).start()
+            to_wave(u, other).start()
             return carry
 
         lax.fori_loop(0, TILES, send_q, 0)
@@ -722,12 +728,11 @@
         results = [pltpu.make_async_copy(A2.at[h], out_o.at[:, hs], out_sem.at[h]) for h, hs in enumerate(halves)]
         for copy in results:
             copy.start()
-        part.wait_send()
         for n in range(2):
             pl.when(has_hi)(edge(n, 0).wait_send)
             pl.when(has_lo)(edge(n, 1).wait_send)
             level(n).wait_send()
-        settle(MSG, q_send)
+        settle(QR, q_send)
         flags.wait()
         for copy in results:
             copy.wait()
@@ -825,12 +830,12 @@
         v(WSTEPS, 2, 2, FD, 128), v(WSTEPS, 2, 2, FD, 128),
         v(2, 8, 256), v(8, 256, dtype=jnp.int32), v(8, 256, dtype=jnp.int32),
         v(16, 256, dtype=jnp.int32), v(2, 16, 256, dtype=jnp.int32),
-        v(256, 128), v(WSTEPS, 8, 256), v(WSTEPS, 5, 8, 256), v(40, 256), v(40, 256), v(256, 128), v(256, 128),
-        v(2, 192, 128), v(2, 192, 128), v(2, 192, 128), v(8, 256), v(16, 256), v(16, 256), v(128, 256),
-        v(256, 128), v(256, 128), v(256, 256),
+        v(2, TILES, 4, 128), v(WSTEPS, 8, 256), v(WSTEPS, 5, 8, 256), v(40, 256), v(40, 256), v(256, 128), v(256, 128),
+        v(2, 192, 128), v(2, 192, 128), v(2, 192, 128), v(8, 256), v(16, 256), v(128, 256),
+        v(TILES, 4, 128), v(256, 128), v(256, 256),
         v(2, 2, 24, 256), v(2, 2, 24, 256), v(2, 24, 256), v(2, 24, 256),
         dma(CHUNKS, 2), dma(3), dma(WSTEPS, 2, CHUNKS), dma(WSTEPS, 2, CHUNKS), dma(WSTEPS, 5), dma(WSTEPS, 5),
-        dma(2), dma(2), dma(), dma(), dma(), dma(), dma(), dma(), dma(), dma(),
+        dma(2), dma(2), dma(), dma(), dma(), dma(), dma(), dma(),
         dma(2, 2), dma(2, 2), dma(2), dma(2), dma(2),
     ]
     landed = pl.pallas_call(

time: 59.3 us -> 57.8 us (0.975)
  Pallas kernels: 58.3 us -> 57 us
    pallas_call x1, Pallas kernels: 55.5 us -> 54.2 us  [body(): pl.pallas_call(kernel, out_shape=(jax.ShapeDtypeStruct((FD * 8, 256), F32...]
where the time goes in v5:
time: 57.8 us; the launch traced here: 57.6 us
  Pallas kernels  57 us (99%)
  between operations  0.64 us (1%)
    pallas_call x1, Pallas kernels, body(): pl.pallas_call(kernel, out_shape=(jax.ShapeDtypeStruct((FD * 8, 256), F32...  54.2 us
    pallas_call x1, Pallas kernels, body(): pl.pallas_call(tail, out_shape=(jax.ShapeDtypeStruct((FD * 8, 256), F32),...  2.77 us

profile of v5, /device:TPU:65, one launch (start us, length us, event | category | flops | bytes accessed | tf_op | source)
XLA Modules:
  0.0 57.6 jit_solution(11032240875440380420)
XLA Ops:
  0.6 54.2 %shard_map.77 = (f32[4608,256]{1,0:T(8,128)S(1)}, f32[192,256]{1,0:T(8,128)S(1)}, f32[256,128]{1,0:T(8,128)S(1)}, f32[256,128]{1,0:T(8,128)S(1)}) custom-call(f32[4608,256]{1,0:T(8,128)} %bitcast.5, f32[2,8,256]{2,1,0:T(8,128)} %wind_h.1, s32[8,256]{1,0:T(8,128)} %land_h.1, s32[8,256]{1,0:T(8,128)} %inter_h.1, f32[192,256]{1,0:T(8,128)} %bitcast.6, ...), custom_call_target="tpu_custom_call" | custom-call | tf_op jit(solution)/shard_map/pallas_call | solution.py:841
  54.8 2.8 %shard_map.78 = (f32[4608,256]{1,0:T(8,128)}, f32[192,256]{1,0:T(8,128)}) custom-call(f32[4608,256]{1,0:T(8,128)S(1)} %get-tuple-element.8.wave_h, f32[192,256]{1,0:T(8,128)S(1)} %get-tuple-element.9.unforced_h, f32[256,128]{1,0:T(8,128)S(1)} %get-tuple-element.10.bands_h, f32[256,128]{1,0:T(8,128)S(1)} %get-tuple-element.11.flags_h), custom_call_target="tpu_custom_call" | custom-call | tf_op jit(solution)/shard_map/pallas_call | solution.py:866

commit v6 on v5

--- a/solution.py
+++ b/solution.py
@@ -87,11 +87,11 @@
 
 
 def kernel(
-    spec_h, wind_h, land_h, inter_h, ocean_h, sea_h, out_w, out_o, BR, out_m,
-    tab, B, G, PT, WD, CNT, H, S, wind, land, inter, NBS, NBR, QR, TS, TR, BANDS, BANDR, MSG2, MMSG,
-    Q, A1, A2, sea, CS, SX, MSG, MR, BTS, ES, EH, LS, LH,
+    spec_h, wind_h, land_h, inter_h, ocean_h, sea_h, out_w, out_o, BR, BT, out_m, out_s,
+    tab, B, G, PT, WD, CNT, H, S, wind, land, inter, NBS, NBR, QR, TS, TR, MSG2, MSG3, MMSG,
+    Q, A1, A2, sea, CS, SX, MSG, MR, BTS, ES, EH, SEA3, LS, LH,
     load_sem, small_sem, h_send, h_recv, t_send, t_recv, nb_send, nb_recv,
-    q_send, q_recv, m_send, m_recv, f_send, f_recv, e_send, e_recv, l_send, l_recv, out_sem,
+    q_send, q_recv, m_send, m_recv, f_send, f_recv, g_send, g_recv, e_send, e_recv, l_send, l_recv, out_sem,
 ):
     grp = lax.axis_index("grp")
     tile = lax.axis_index("tile")
@@ -115,9 +115,22 @@
         return jnp.where(m, b, a), jnp.where(m, a, b)
 
     def barrel(x, amount):
-        for bit in range(8):
-            moved = circular(x, 1 << bit) if bit < 7 else (x[1], x[0])
-            x = tuple(jnp.where((amount[h] & (1 << bit)) != 0, moved[h], x[h]) for h in range(2))
+        for bit in range(0, 8, 2):
+            options = [x]
+            for digit in range(1, 4):
+                by = digit << bit
+                y = circular(x, by % 128) if by % 128 else x
+                options.append((y[1], y[0]) if by >= 128 else y)
+            low = [(amount[h] & (1 << bit)) != 0 for h in range(2)]
+            high = [(amount[h] & (2 << bit)) != 0 for h in range(2)]
+            x = tuple(
+                jnp.where(
+                    high[h],
+                    jnp.where(low[h], options[3][h], options[2][h]),
+                    jnp.where(low[h], options[1][h], options[0][h]),
+                )
+                for h in range(2)
+            )
         return x
 
     def pair(ref, *lead):
@@ -231,23 +244,23 @@
 
         wet_back = circular(barrel(wet, shift), 1)
 
-        def windows(fields, u):
+        def windows(fields, u, pitch):
             acc = jnp.zeros((8, 128), F32)
             for f, field in enumerate(fields):
-                start = (8 * u + 32 * f) % 128
+                start = (8 * u + pitch * f) % 128
                 offset = (lane - start) & 127
                 inside = offset < 10
                 base = (8 * u) // 128
                 p = 8 * u + offset
                 value = field[base]
                 if 8 * u % 128 + 10 > 128:
-                    turned = (lane - 32 * f) & 127
+                    turned = (lane - pitch * f) & 127
                     value = jnp.where(turned < 16, field[1 - base], value)
                 acc = jnp.where(inside, value, acc)
             return acc
 
         for u in range(TILES):
-            MMSG[pl.ds(8 * u, 8), :] = windows([wet_back], u)
+            MMSG[pl.ds(8 * u, 8), :] = windows([wet_back], u, 32)
 
         def to_ocean(src, dst, send, recv, u):
             return mesh_copy(
@@ -528,27 +541,33 @@
         r, edge_r = lax.fori_loop(0, WSTEPS - 1, one_step, (wet, edge_wet))
         n = WSTEPS - 1
         sums = sweep(n, r, edge_r, True)
-        for q in range(5):
-            put(BANDS, sums[q], slice(8 * q, 8 * q + 8))
-        swap = mesh_copy(BANDS, BANDR, t_send.at[n, 0], t_recv.at[n, 0], {"spec": other})
+        for h, hs in enumerate(halves):
+            TS[n, :, hs] = sums[0][h]
+        swap = mesh_copy(TS.at[n], TR.at[n, 0], t_send.at[n, 0], t_recv.at[n, 0], {"spec": other})
         swap.start()
+        turned = [circular(barrel(sums[q], shift), 1) for q in (0, 3, 4, 1, 2)]
+        slots = [tuple(pltpu.roll(x, 16 * f, 1) if f else x for x in field) for f, field in enumerate(turned[:4])]
+        slot = lax.broadcasted_iota(jnp.int32, (4, 128), 1) < 64
+        for fields, out in ((slots, MSG2), (turned[4:], MSG3)):
+            for u in range(TILES):
+                wide = windows(fields, u, 16)
+                wide = wide + pltpu.roll(wide, 64, 1)
+                out[u] = jnp.where(slot, wide[0:4], wide[4:8])
+
+        def bands_to(src, dst, send, recv, u, half):
+            return mesh_copy(src.at[u], dst.at[sp, tile], send, recv, {"grp": 1, "tile": u, "spec": half})
+
+        def send_bands(u, carry):
+            bands_to(MSG2, BR, f_send, f_recv, u, sp).start()
+            bands_to(MSG2, BR, f_send, f_recv, u, other).start()
+            bands_to(MSG3, BT, g_send, g_recv, u, 0).start()
+            return carry
+
+        lax.fori_loop(0, TILES, send_bands, 0)
         swap.wait_recv()
-        full = [tuple(sums[q][h] + BANDR[8 * q : 8 * q + 8, halves[h]] for h in range(2)) for q in range(5)]
-        breaking = tuple(1.0 / (1.0 + stiff[h] * full[0][h]) for h in range(2))
-        final = tuple(wet[h] * breaking[h] for h in range(2))
-        bands = []
-        for q in range(1, 5):
-            scale = breaking if q < 3 else final
-            bands.append(circular(barrel(tuple(scale[h] * full[q][h] for h in range(2)), shift), 1))
-        bands = [tuple(pltpu.roll(x, 32 * f, 1) if f else x for x in field) for f, field in enumerate(bands)]
-        for u in range(TILES):
-            MSG2[pl.ds(8 * u, 8), :] = windows(bands, u)
-
-        def send_bands(u, carry):
-            to_ocean(MSG2, BR, f_send, f_recv, u).start()
-            return carry
-
-        lax.fori_loop(0, TILES, send_bands, 0)
+        final = tuple(
+            wet[h] / (1.0 + stiff[h] * (sums[0][h] + TR[n, 0, :, halves[h]])) for h in range(2)
+        )
 
         def store(c):
             rows = pl.ds(pl.multiple_of(c * RCH * 8, 8), RCH * 8)
@@ -595,7 +614,8 @@
         gated(has_hi, neighbour(0).wait_send)
         gated(has_lo, neighbour(1).wait_send)
         settle(MMSG, m_send)
-        settle(MSG2, f_send)
+        settle(BR, f_send)
+        settle(MSG3, g_send)
 
     @pl.when(grp == 1)
     def circulation():
@@ -635,6 +655,8 @@
                     LS[n, pl.ds(8 * c, 8), hs] = jnp.where(
                         sp == 0, src[h, pl.ds(c * 64 + 56, 8), :], src[h, pl.ds(c * 64, 8), :]
                     )
+            for side in range(2):
+                ES[n, side, 24:32, :] = sea[...]
             pl.when(has_hi)(edge(n, 0).start)
             pl.when(has_lo)(edge(n, 1).start)
             level(n).start()
@@ -671,11 +693,11 @@
 
         @pl.when(jnp.logical_not(has_lo))
         def _():
-            EH[:, 0] = jnp.zeros((2, 24, 256), F32)
+            EH[:, 0] = jnp.zeros((2, 32, 256), F32)
 
         @pl.when(jnp.logical_not(has_hi))
         def _():
-            EH[:, 1] = jnp.zeros((2, 24, 256), F32)
+            EH[:, 1] = jnp.zeros((2, 32, 256), F32)
 
         settle(MR, m_recv)
         flags = pltpu.make_async_copy(MR, out_m, small_sem.at[0])
@@ -720,6 +742,13 @@
             level(n).wait_recv()
 
         rims_in(0)
+        for h, hs in enumerate(halves):
+            level_here = sea[:, hs]
+            SEA3[0:8, hs] = jnp.where(first_row, EH[0, 0, 31:32, hs], pltpu.roll(level_here, 1, 0))
+            SEA3[8:16, hs] = level_here
+            SEA3[16:24, hs] = jnp.where(last_row, EH[0, 1, 24:25, hs], pltpu.roll(level_here, 7, 0))
+        seas = pltpu.make_async_copy(SEA3, out_s, small_sem.at[1])
+        seas.start()
         substep(0, Q, A1)
         rims_out(1, A1)
         rims_in(1)
@@ -734,12 +763,14 @@
             level(n).wait_send()
         settle(QR, q_send)
         flags.wait()
+        seas.wait()
         for copy in results:
             copy.wait()
         settle(BR, f_recv)
-
-
-def tail(wave_h, unforced_h, bands_h, flags_h, out_w, out_o, zeros, A2, BR, MR, BTS, in_sem, w_sem, o_sem):
+        pl.when(sp == 0)(lambda: settle(BT, g_recv))
+
+
+def tail(wave_h, unforced_h, bands_h, north_h, flags_h, sea_h, out_w, out_o, zeros, A2, BR, BT, MR, U, sea, BTS, in_sem, w_sem, o_sem):
     grp = lax.axis_index("grp")
     tile = lax.axis_index("tile")
     sp = lax.axis_index("spec")
@@ -762,9 +793,16 @@
         loads = [
             pltpu.make_async_copy(flags_h, MR, in_sem.at[0]),
             pltpu.make_async_copy(bands_h, BR, in_sem.at[1]),
+            pltpu.make_async_copy(sea_h, sea, in_sem.at[4]),
         ] + [pltpu.make_async_copy(unforced_h.at[:, hs], A2.at[h], in_sem.at[2 + h]) for h, hs in enumerate(HALVES)]
         for copy in loads:
             copy.start()
+        norths = pltpu.make_async_copy(north_h, BT, in_sem.at[5])
+
+        @pl.when(sp == 0)
+        def _():
+            norths.start()
+
         zeros[...] = jnp.zeros(zeros.shape, F32)
         blanks = []
         for c in range(CHUNKS):
@@ -784,11 +822,42 @@
         mask_hi = tuple(jnp.where(row == 7, x[2] * at_hi, x[2]) for x in mask3)
         for copy in loads[1:]:
             copy.wait()
+
+        @pl.when(sp == 0)
+        def _():
+            norths.wait()
+
+        @pl.when(sp == 1)
+        def _():
+            BT[...] = jnp.zeros(BT.shape, F32)
+
+        def unpacked(buf, slots):
+            for t in range(TILES):
+                both = buf[0, t] + buf[1, t]
+                U[8 * t : 8 * t + 8, :] = jnp.concatenate([both, pltpu.roll(both, 64, 1)], axis=0)
+            for h in range(2):
+                turned = U[pl.ds(128 * h, 128), :].T
+                BTS[pl.ds(0, 64), HALVES[h]] = turned[0:64]
+                BTS[pl.ds(64, 64), HALVES[h]] = turned[0:64]
+            out = []
+            for f in range(slots):
+                start = pl.multiple_of((8 * tile + 16 * f) % 64, 8)
+                wide = BTS[pl.ds(start, 16), :]
+                out.append(tuple((wide[0:8, hs], wide[1:9, hs], wide[2:10, hs]) for hs in HALVES))
+            return out
+
+        total, drift_e, drift_n, stress_e = unpacked(BR, 4)
+        (stress_n,) = unpacked(BT, 1)
+        factor = []
+        for h, hs in enumerate(HALVES):
+            row_of = []
+            for q, masked in enumerate((mask_lo, mask, mask_hi)):
+                depth = 10.0 + 4.0 * sea[8 * q : 8 * q + 8, hs]
+                row_of.append(masked[h] / (1.0 + 25.0 * total[h][q] / (depth * depth)))
+            factor.append(row_of)
         forced, spread = [], []
-        for f, three in enumerate(arrived(BR, BTS, tile, 4)):
-            lower = tuple(three[h][0] * mask_lo[h] for h in range(2))
-            own = tuple(three[h][1] * mask[h] for h in range(2))
-            upper = tuple(three[h][2] * mask_hi[h] for h in range(2))
+        for three in (stress_e, stress_n, drift_e, drift_n):
+            lower, own, upper = (tuple(three[h][q] * factor[h][q] for h in range(2)) for q in range(3))
             forced.append(own)
             spread.append(lateral(own, lower, upper))
         for k in range(KLOC):
@@ -830,12 +899,12 @@
         v(WSTEPS, 2, 2, FD, 128), v(WSTEPS, 2, 2, FD, 128),
         v(2, 8, 256), v(8, 256, dtype=jnp.int32), v(8, 256, dtype=jnp.int32),
         v(16, 256, dtype=jnp.int32), v(2, 16, 256, dtype=jnp.int32),
-        v(2, TILES, 4, 128), v(WSTEPS, 8, 256), v(WSTEPS, 5, 8, 256), v(40, 256), v(40, 256), v(256, 128), v(256, 128),
+        v(2, TILES, 4, 128), v(WSTEPS, 8, 256), v(WSTEPS, 5, 8, 256), v(TILES, 4, 128), v(TILES, 4, 128), v(256, 128),
         v(2, 192, 128), v(2, 192, 128), v(2, 192, 128), v(8, 256), v(16, 256), v(128, 256),
         v(TILES, 4, 128), v(256, 128), v(256, 256),
-        v(2, 2, 24, 256), v(2, 2, 24, 256), v(2, 24, 256), v(2, 24, 256),
+        v(2, 2, 32, 256), v(2, 2, 32, 256), v(24, 256), v(2, 24, 256), v(2, 24, 256),
         dma(CHUNKS, 2), dma(3), dma(WSTEPS, 2, CHUNKS), dma(WSTEPS, 2, CHUNKS), dma(WSTEPS, 5), dma(WSTEPS, 5),
-        dma(2), dma(2), dma(), dma(), dma(), dma(), dma(), dma(),
+        dma(2), dma(2), dma(), dma(), dma(), dma(), dma(), dma(), dma(), dma(),
         dma(2, 2), dma(2, 2), dma(2), dma(2), dma(2),
     ]
     landed = pl.pallas_call(
@@ -843,11 +912,13 @@
         out_shape=(
             jax.ShapeDtypeStruct((FD * 8, 256), F32),
             jax.ShapeDtypeStruct((192, 256), F32),
+            jax.ShapeDtypeStruct((2, TILES, 4, 128), F32),
+            jax.ShapeDtypeStruct((2, TILES, 4, 128), F32),
             jax.ShapeDtypeStruct((256, 128), F32),
-            jax.ShapeDtypeStruct((256, 128), F32),
+            jax.ShapeDtypeStruct((24, 256), F32),
         ),
         in_specs=[anywhere] * 6,
-        out_specs=(pl.BlockSpec(memory_space=pl.ANY),) * 4,
+        out_specs=(pl.BlockSpec(memory_space=pl.ANY),) * 6,
         scratch_shapes=scratch,
         compiler_params=pltpu.CompilerParams(collective_id=0, has_side_effects=True, vmem_limit_bytes=48 << 20),
     )(
@@ -866,10 +937,11 @@
     waves, ocean = pl.pallas_call(
         tail,
         out_shape=(jax.ShapeDtypeStruct((FD * 8, 256), F32), jax.ShapeDtypeStruct((192, 256), F32)),
-        in_specs=[pl.BlockSpec(memory_space=pl.ANY)] * 4,
+        in_specs=[pl.BlockSpec(memory_space=pl.ANY)] * 6,
         out_specs=(pl.BlockSpec(memory_space=pl.ANY),) * 2,
         scratch_shapes=[
-            v(RCH * 8, 256), v(2, 192, 128), v(256, 128), v(256, 128), v(256, 256), dma(4), dma(CHUNKS), dma(2)
+            v(RCH * 8, 256), v(2, 192, 128), v(2, TILES, 4, 128), v(2, TILES, 4, 128), v(256, 128), v(256, 128),
+            v(24, 256), v(256, 256), dma(6), dma(CHUNKS), dma(2),
         ],
         compiler_params=pltpu.CompilerParams(vmem_limit_bytes=6 << 20),
     )(*landed)

time: 57.8 us -> 55.3 us (0.957)
  Pallas kernels: 57 us -> 54.5 us
    pallas_call x1, Pallas kernels: 54.2 us -> 51.6 us  [body(): pl.pallas_call(kernel, out_shape=(jax.ShapeDtypeStruct((FD * 8, 256), F32...]
where the time goes in v6:
time: 55.3 us; the launch traced here: 55.2 us
  Pallas kernels  54.5 us (99%)
  between operations  0.64 us (1%)
    pallas_call x1, Pallas kernels, body(): pl.pallas_call(kernel, out_shape=(jax.ShapeDtypeStruct((FD * 8, 256), F32...  51.6 us
    pallas_call x1, Pallas kernels, body(): pl.pallas_call(tail, out_shape=(jax.ShapeDtypeStruct((FD * 8, 256), F32),...  2.99 us

profile of v6, /device:TPU:65, one launch (start us, length us, event | category | flops | bytes accessed | tf_op | source)
XLA Modules:
  0.0 55.2 jit_solution(2181403774185820242)
XLA Ops:
  0.6 51.6 %shard_map.77 = (f32[4608,256]{1,0:T(8,128)S(1)}, f32[192,256]{1,0:T(8,128)S(1)}, f32[2,32,4,128]{3,2,1,0:T(4,128)S(1)}, f32[2,32,4,128]{3,2,1,0:T(4,128)S(1)}, ...) custom-call(f32[4608,256]{1,0:T(8,128)} %bitcast.5, f32[2,8,256]{2,1,0:T(8,128)} %wind_h.1, s32[8,256]{1,0:T(8,128)} %land_h.1, ...), custom_call_target="tpu_custom_call" | custom-call | tf_op jit(solution)/shard_map/pallas_call | solution.py:910
  52.2 3.0 %shard_map.78 = (f32[4608,256]{1,0:T(8,128)}, f32[192,256]{1,0:T(8,128)}) custom-call(f32[4608,256]{1,0:T(8,128)S(1)} %get-tuple-element.10.wave_h, f32[192,256]{1,0:T(8,128)S(1)} %get-tuple-element.11.unforced_h, f32[2,32,4,128]{3,2,1,0:T(4,128)S(1)} %get-tuple-element.12.bands_h, f32[2,32,4,128]{3,2,1,0:T(4,128)S(1)} %get-tuple-element.13.north_h, ...), custom_call_target="tpu_custom_call" | custom-call | tf_op jit(solution)/shard_map/pallas_call | solution.py:937

commit v7 on v6

--- a/solution.py
+++ b/solution.py
@@ -19,8 +19,8 @@
 CHUNKS = 8
 FCH = FREQS // CHUNKS
 RCH = FCH * DLOC
-PCH = 5
-HELD = 3
+PCH = 4
+HELD = 4
 F32 = jnp.float32
 
 _freq = 0.04 * 1.1 ** np.arange(FREQS)

time: 55.3 us -> 53.7 us (0.971)
  Pallas kernels: 54.5 us -> 52.9 us
    pallas_call x1, Pallas kernels: 51.6 us -> 49.9 us  [body(): pl.pallas_call(kernel, out_shape=(jax.ShapeDtypeStruct((FD * 8, 256), F32...]
where the time goes in v7:
time: 53.7 us; the launch traced here: 53.5 us
  Pallas kernels  52.9 us (99%)
  between operations  0.64 us (1%)
    pallas_call x1, Pallas kernels, body(): pl.pallas_call(kernel, out_shape=(jax.ShapeDtypeStruct((FD * 8, 256), F32...  49.9 us
    pallas_call x1, Pallas kernels, body(): pl.pallas_call(tail, out_shape=(jax.ShapeDtypeStruct((FD * 8, 256), F32),...  2.99 us

profile of v7, /device:TPU:65, one launch (start us, length us, event | category | flops | bytes accessed | tf_op | source)
XLA Modules:
  0.0 53.5 jit_solution(9018427361042833897)
XLA Ops:
  0.6 49.9 %shard_map.77 = (f32[4608,256]{1,0:T(8,128)S(1)}, f32[192,256]{1,0:T(8,128)S(1)}, f32[2,32,4,128]{3,2,1,0:T(4,128)S(1)}, f32[2,32,4,128]{3,2,1,0:T(4,128)S(1)}, ...) custom-call(f32[4608,256]{1,0:T(8,128)} %bitcast.5, f32[2,8,256]{2,1,0:T(8,128)} %wind_h.1, s32[8,256]{1,0:T(8,128)} %land_h.1, ...), custom_call_target="tpu_custom_call" | custom-call | tf_op jit(solution)/shard_map/pallas_call | solution.py:910
  50.5 3.0 %shard_map.78 = (f32[4608,256]{1,0:T(8,128)}, f32[192,256]{1,0:T(8,128)}) custom-call(f32[4608,256]{1,0:T(8,128)S(1)} %get-tuple-element.10.wave_h, f32[192,256]{1,0:T(8,128)S(1)} %get-tuple-element.11.unforced_h, f32[2,32,4,128]{3,2,1,0:T(4,128)S(1)} %get-tuple-element.12.bands_h, f32[2,32,4,128]{3,2,1,0:T(4,128)S(1)} %get-tuple-element.13.north_h, ...), custom_call_target="tpu_custom_call" | custom-call | tf_op jit(solution)/shard_map/pallas_call | solution.py:937

commit v8 on v7

--- a/solution.py
+++ b/solution.py
@@ -484,7 +484,7 @@
                 sums = lax.fori_loop(0, FCH, band, sums, unroll=2)
                 if not last:
 
-                    @pl.when(c < CHUNKS - HELD)
+                    @pl.when(c < CHUNKS - jnp.where(n > 0, HELD, HELD - 1))
                     def _():
                         edges_out(n + 1, c)
 
@@ -524,7 +524,7 @@
                 edges_out(n + 1, c)
                 return carry
 
-            lax.fori_loop(CHUNKS - HELD, CHUNKS, late, 0)
+            lax.fori_loop(CHUNKS - jnp.where(n > 0, HELD, HELD - 1), CHUNKS, late, 0)
             ahead(n + 1)
             for (_, copy), condition in zip(copies, [None, has_lo, has_lo, has_hi, has_hi]):
                 gated(condition, copy.wait_recv)

time: 53.7 us -> 54.3 us (1.011)
  Pallas kernels: 52.9 us -> 53.5 us
    pallas_call x1, Pallas kernels: 49.9 us -> 50.5 us  [body(): pl.pallas_call(kernel, out_shape=(jax.ShapeDtypeStruct((FD * 8, 256), F32...]
where the time goes in v8:
time: 54.3 us; the launch traced here: 54.2 us
  Pallas kernels  53.5 us (99%)
  between operations  0.64 us (1%)
    pallas_call x1, Pallas kernels, body(): pl.pallas_call(kernel, out_shape=(jax.ShapeDtypeStruct((FD * 8, 256), F32...  50.5 us
    pallas_call x1, Pallas kernels, body(): pl.pallas_call(tail, out_shape=(jax.ShapeDtypeStruct((FD * 8, 256), F32),...  2.99 us

profile of v8, /device:TPU:65, one launch (start us, length us, event | category | flops | bytes accessed | tf_op | source)
XLA Modules:
  0.0 54.2 jit_solution(9710786132922611751)
XLA Ops:
  0.6 50.5 %shard_map.77 = (f32[4608,256]{1,0:T(8,128)S(1)}, f32[192,256]{1,0:T(8,128)S(1)}, f32[2,32,4,128]{3,2,1,0:T(4,128)S(1)}, f32[2,32,4,128]{3,2,1,0:T(4,128)S(1)}, ...) custom-call(f32[4608,256]{1,0:T(8,128)} %bitcast.5, f32[2,8,256]{2,1,0:T(8,128)} %wind_h.1, s32[8,256]{1,0:T(8,128)} %land_h.1, ...), custom_call_target="tpu_custom_call" | custom-call | tf_op jit(solution)/shard_map/pallas_call | solution.py:910
  51.2 3.0 %shard_map.78 = (f32[4608,256]{1,0:T(8,128)}, f32[192,256]{1,0:T(8,128)}) custom-call(f32[4608,256]{1,0:T(8,128)S(1)} %get-tuple-element.10.wave_h, f32[192,256]{1,0:T(8,128)S(1)} %get-tuple-element.11.unforced_h, f32[2,32,4,128]{3,2,1,0:T(4,128)S(1)} %get-tuple-element.12.bands_h, f32[2,32,4,128]{3,2,1,0:T(4,128)S(1)} %get-tuple-element.13.north_h, ...), custom_call_target="tpu_custom_call" | custom-call | tf_op jit(solution)/shard_map/pallas_call | solution.py:937
